TPU v7x, 256 devices: a whole 4x4x8 slice. The times are simulated.
256 devices in a mesh: head: 4 (over x), batch: 64 (over y, z, core).
Axes of the slice: x: 4, y: 4, z: 8, core: 2. Of those that a mesh axis runs over, the one named last changes fastest.
Arguments:
- query_symbol_numbers: int32 [64, 4], P('batch'), may hold values from 0 to 65535
- alive_span_sizes: int32 [64], P('batch'), may hold values from 1 to 4
- former_positions: int32 [64], P('batch'), may hold values from 0 to 63, each once
- previous_normed_vectors: bfloat16 [2, 64, 4096], P(None, 'batch'), may hold values from -6 to 6
- memory_matrices: bfloat16 [64, 64, 64, 64], P('batch', 'head'), may hold values from -6 to 6
- vocabulary_vectors: bfloat16 [4096, 65536], P('batch', 'head'), may hold values from -6 to 6
- standardize_scales: float32 [2, 4096], P(None, 'batch'), may hold values from 0.5 to 1.5
- standardize_shifts: float32 [2, 4096], P(None, 'batch'), may hold values from -2 to 2
- timemix_blend_factors: float32 [5, 4096], P(None, 'batch'), may hold values from 0 to 1
- timemix_linear_maps: bfloat16 [4, 4096, 4096], P(None, 'batch', 'head'), may hold values from -0.09375 to 0.09375
- forgetting_first_lowrank: bfloat16 [4096, 128], P('batch'), may hold values from -0.09375 to 0.09375
- forgetting_second_lowrank: bfloat16 [128, 4096], P(None, 'head'), may hold values from -0.5 to 0.5
- forgetting_loglog_floor: float32 [4096], P('head'), may hold values from -6 to 0
- current_reward_factor: float32 [4096], P('head'), may hold values from -3 to 3
- perspan_standardize_scale: float32 [4096], P('head'), may hold values from 0.5 to 1.5
- perspan_standardize_shift: float32 [4096], P('head'), may hold values from -2 to 2
- timemix_emit_matrix: bfloat16 [4096, 4096], P('batch', 'head'), may hold values from -0.09375 to 0.09375
- feedforward_blend_factors: float32 [2, 4096], P(None, 'batch'), may hold values from 0 to 1
- feedforward_lookup_matrix: bfloat16 [4096, 14336], P('batch', 'head'), may hold values from -0.09375 to 0.09375
- feedforward_accept_matrix: bfloat16 [4096, 4096], P('batch'), may hold values from -0.09375 to 0.09375
- feedforward_emit_matrix: bfloat16 [4096, 14336], P('batch', 'head'), may hold values from -0.046875 to 0.046875
Outputs:
- hidden: float32 [64, 4, 4096], P(None, None, 'batch')
- new_edges: bfloat16 [2, 64, 4096], P(None, None, 'batch')
- new_states: bfloat16 [64, 64, 64, 64], P('batch', 'head')
Inputs may be any that keep to these rules, and one draw needn't show every extreme that they name: `alive_span_sizes`: some request has 4 live tokens. `former_positions`: each old index appears exactly once.
All inputs are finite; a program needn't handle non-finite values.
Results may differ from a plain program's by a relative error of at most 0.015.
Values may be sent and summed in bfloat16 or wider, within the bound.
A program may use at most 128 MiB of HBM per device.

v0:
```python
import jax
import jax.numpy as jnp
from jax import lax
from jax.sharding import PartitionSpec as P

EMBEDDING_DIM = 4096


EPS_LN = 1e-05
EPS_GN = 0.00064


def normalize(stream, gain, bias):
    mean = lax.psum(jnp.sum(stream, axis=-1), "batch") / EMBEDDING_DIM
    centered = stream - mean[..., None]
    spread = lax.psum(jnp.sum(centered * centered, axis=-1), "batch") / EMBEDDING_DIM
    scaled = (stream - mean[..., None]) * lax.rsqrt(spread[..., None] + EPS_LN)
    return (scaled * gain + bias).astype(jnp.bfloat16)


def shifted(normed, edge, mixes):
    before = jnp.concatenate([edge[:, None], normed[:, :-1]], axis=1)
    delta = before.astype(jnp.float32) - normed.astype(jnp.float32)
    return (normed.astype(jnp.float32)[None] + delta[None] * mixes[:, None, None, :]).astype(
        jnp.bfloat16
    )


def local(
    query_symbol_numbers,
    alive_span_sizes,
    former_positions,
    previous_normed_vectors,
    memory_matrices,
    vocabulary_vectors,
    standardize_scales,
    standardize_shifts,
    timemix_blend_factors,
    timemix_linear_maps,
    forgetting_first_lowrank,
    forgetting_second_lowrank,
    forgetting_loglog_floor,
    current_reward_factor,
    perspan_standardize_scale,
    perspan_standardize_shift,
    timemix_emit_matrix,
    feedforward_blend_factors,
    feedforward_lookup_matrix,
    feedforward_accept_matrix,
    feedforward_emit_matrix,
):
    req_local, slots = query_symbol_numbers.shape
    ids_all, lengths_all, owners_all = (
        lax.all_gather(query_symbol_numbers, "batch", axis=0, tiled=True),
        lax.all_gather(alive_span_sizes, "batch", axis=0, tiled=True),
        lax.all_gather(former_positions, "batch", axis=0, tiled=True),
    )
    requests = ids_all.shape[0]
    count = requests * slots
    tok_local = req_local * slots
    width_local = standardize_scales.shape[1]
    vocab_local = vocabulary_vectors.shape[1]
    offset = ids_all - lax.axis_index("head") * vocab_local
    inside = (offset >= 0) & (offset < vocab_local)
    looked = jnp.moveaxis(
        jnp.take(vocabulary_vectors, jnp.clip(offset, 0, vocab_local - 1), axis=1), 0, -1
    )
    stream = lax.psum(
        jnp.where(inside[..., None], looked.astype(jnp.float32), 0.0).astype(jnp.bfloat16), "head"
    ).astype(jnp.float32)
    moved = lax.all_to_all(
        previous_normed_vectors, "batch", split_axis=2, concat_axis=1, tiled=True
    )
    edges = jnp.take(moved, owners_all, axis=1)
    subspace_total_here, subspace_size_here = (memory_matrices.shape[1], memory_matrices.shape[2])
    state_width = subspace_total_here * subspace_size_here * subspace_size_here
    first_mine = lax.axis_index("batch") * req_local
    mine = lax.dynamic_slice_in_dim(owners_all, first_mine, req_local)
    piece = lax.all_gather(memory_matrices, "batch", axis=0, tiled=True)
    rows = piece.shape[0]
    select = (mine[:, None] == jnp.arange(rows, dtype=jnp.int32)[None, :]).astype(jnp.bfloat16)
    begun = jnp.dot(select, piece.reshape(rows, state_width), preferred_element_type=jnp.float32)
    memory_collection = begun.reshape(
        req_local, subspace_total_here, subspace_size_here, subspace_size_here
    )
    normed = normalize(stream, standardize_scales[0], standardize_shifts[0])
    mixed = shifted(normed, edges[0], timemix_blend_factors).reshape(5, count, width_local)
    cols = timemix_linear_maps.shape[2]
    part = mixed
    main = jnp.einsum(
        "ntd,nde->tne", part[:4], timemix_linear_maps, preferred_element_type=jnp.float32
    ).reshape(lax.axis_size("batch") * tok_local, 4 * cols)
    lowpart = jnp.dot(part[4], forgetting_first_lowrank, preferred_element_type=jnp.float32)
    proj = lax.psum_scatter(
        jnp.concatenate([main, lowpart], axis=1), "batch", scatter_dimension=0, tiled=True
    )
    main = proj[:, : 4 * cols].reshape(tok_local, 4, cols)
    low = jnp.tanh(proj[:, 4 * cols :]).astype(jnp.bfloat16)
    decay = jnp.exp(
        -jnp.exp(
            forgetting_loglog_floor
            + jnp.dot(low, forgetting_second_lowrank, preferred_element_type=jnp.float32)
        )
    )
    shape = (req_local, slots, subspace_total_here, subspace_size_here)
    arriving_memories = main[:, 0].reshape(shape)
    key = main[:, 1].reshape(shape)
    value = main[:, 2].reshape(shape)
    gate = main[:, 3]
    decay = decay.reshape(shape)
    subspace_reward_contribution = current_reward_factor.reshape(
        subspace_total_here, subspace_size_here
    )
    carry = (memory_collection, jnp.zeros(shape, jnp.float32))
    for position_number in range(slots):
        current_symbol, result_vectors = carry
        receptance_present = lax.dynamic_index_in_dim(
            arriving_memories, position_number, 1, keepdims=False
        )
        k_now = lax.dynamic_index_in_dim(key, position_number, 1, keepdims=False)
        v_now = lax.dynamic_index_in_dim(value, position_number, 1, keepdims=False)
        d_now = lax.dynamic_index_in_dim(decay, position_number, 1, keepdims=False)
        dyadic_matrix = jnp.einsum("rhk,rhv->rhkv", k_now, v_now)
        output_present = jnp.einsum(
            "tqe,tqeh->tqh",
            receptance_present,
            current_symbol + subspace_reward_contribution[None, :, :, None] * dyadic_matrix,
        )
        alive = (position_number < alive_span_sizes)[:, None, None, None]
        current_symbol = jnp.where(
            alive, d_now[..., None] * current_symbol + dyadic_matrix, current_symbol
        )
        result_vectors = lax.dynamic_update_index_in_dim(
            result_vectors, output_present, position_number, 1
        )
        carry = (current_symbol, result_vectors)
    memory_collection, wkv = carry
    mean = jnp.mean(wkv, axis=-1, keepdims=True)
    spread = jnp.mean(jnp.square(wkv - mean), axis=-1, keepdims=True)
    grouped = ((wkv - mean) * lax.rsqrt(spread + EPS_GN)).reshape(
        tok_local, cols
    ) * perspan_standardize_scale + perspan_standardize_shift
    gated = (grouped * jax.nn.silu(gate)).astype(jnp.bfloat16)
    attended = lax.dot_general(
        lax.all_gather(gated, "batch", axis=0, tiled=True),
        timemix_emit_matrix,
        (((1,), (1,)), ((), ())),
        preferred_element_type=jnp.float32,
    )
    attended = lax.psum(attended.astype(jnp.bfloat16), "head").astype(jnp.float32)
    stream = stream + attended.reshape(requests, slots, width_local)
    normed_two = normalize(stream, standardize_scales[1], standardize_shifts[1])
    mixed_two = shifted(normed_two, edges[1], feedforward_blend_factors).reshape(
        2, count, width_local
    )
    part = mixed_two[0]
    units = jnp.square(
        jax.nn.relu(
            lax.psum_scatter(
                jnp.dot(part, feedforward_lookup_matrix, preferred_element_type=jnp.float32),
                "batch",
                scatter_dimension=0,
                tiled=True,
            )
        )
    ).astype(jnp.bfloat16)
    part = feedforward_accept_matrix
    receive = jax.nn.sigmoid(
        lax.psum_scatter(
            lax.dot_general(
                part, mixed_two[1], (((0,), (1,)), ((), ())), preferred_element_type=jnp.float32
            ),
            "batch",
            scatter_dimension=0,
            tiled=True,
        )
    ).T
    values = lax.dot_general(
        lax.all_gather(units, "batch", axis=0, tiled=True),
        feedforward_emit_matrix,
        (((1,), (1,)), ((), ())),
        preferred_element_type=jnp.float32,
    )
    values = lax.psum(values.astype(jnp.bfloat16), "head").astype(jnp.float32)
    result = stream + (receive * values).reshape(requests, slots, width_local)
    live = jnp.arange(slots, dtype=jnp.int32)[None, :] < lengths_all[:, None]
    hidden = jnp.where(live[..., None], result, jnp.float32(0.0))
    last = (lengths_all - 1)[:, None, None]
    new_edges = jnp.stack(
        [
            jnp.take_along_axis(normed, last, axis=1)[:, 0],
            jnp.take_along_axis(normed_two, last, axis=1)[:, 0],
        ]
    )
    return (hidden, new_edges, memory_collection.astype(jnp.bfloat16))


def solution(mesh):
    return jax.shard_map(
        local,
        mesh=mesh,
        in_specs=(
            P("batch", None),
            P("batch"),
            P("batch"),
            P(None, "batch", None),
            P("batch", "head", None, None),
            P("batch", "head"),
            P(None, "batch"),
            P(None, "batch"),
            P(None, "batch"),
            P(None, "batch", "head"),
            P("batch", None),
            P(None, "head"),
            P("head"),
            P("head"),
            P("head"),
            P("head"),
            P("batch", "head"),
            P(None, "batch"),
            P("batch", "head"),
            P("batch", None),
            P("batch", "head"),
        ),
        out_specs=(P(None, None, "batch"), P(None, None, "batch"), P("batch", "head", None, None)),
        check_vma=False,
    )
```

profile of v0, /device:TPU:1, one launch (start us, length us, event | category | flops | bytes accessed | tf_op | source)
XLA Modules:
  0.0 1985.9 jit_solution(9614757644628712452)
XLA Ops:
  7.2 4.9 copy.119
  12.1 13.2 all-to-all-start
  28.8 55.7 %all-reduce.5 = (s32[64]{0:T(128)S(1)}, s32[64]{0:T(128)S(1)}) all-reduce(s32[64]{0:T(128)S(1)} %dynamic-update-slice.1, s32[64]{0:T(128)S(1)} %dynamic-update-slice), channel_id=1, replica_groups=mesh['head'=4,'batch'=64] {'batch'}, use_global_device_ids=true, to_apply=%add.2 | all-reduce | flops 128 | bytes 1024
  84.5 43.0 %all-gather = s32[64,1,4]{2,1,0:T(1,128)S(1)} all-gather(s32[1,1,4]{2,1,0:T(1,128)S(1)} %bitcast.245), channel_id=1, replica_groups=mesh['head'=4,'batch'=64] {'batch'}, dimensions={0}, use_global_device_ids=true | all-gather | bytes 1040 | tf_op jit(solution)/shard_map/all_gather | solution.py:54
  128.1 4.8 copy.118
  136.6 13.8 psum.49
  150.5 244.4 %psum.50 = f32[64,4]{1,0:T(8,128)S(1)} all-reduce(f32[64,4]{1,0:T(8,128)S(1)} %convert_reduce_fusion), channel_id=1, replica_groups=mesh['head'=4,'batch'=64] {'batch'}, use_global_device_ids=true, to_apply=%region_2.3 | all-reduce | flops 256 | bytes 2048 | tf_op jit(solution)/shard_map/psum | solution.py:14
  395.2 246.1 %psum.51 = f32[64,4]{1,0:T(8,128)S(1)} all-reduce(f32[64,4]{1,0:T(8,128)S(1)} %fusion.47), channel_id=1, replica_groups=mesh['head'=4,'batch'=64] {'batch'}, use_global_device_ids=true, to_apply=%region_4.5 | all-reduce | flops 256 | bytes 2048 | tf_op jit(solution)/shard_map/psum | solution.py:16
  647.6 5.4 copy.124
  653.2 4.4 pad_maximum_fusion
  660.0 189.1 %all-reduce.9.cloned.1.call-done = f32[256,4224]{0,1:T(8,128)} async-done(((f32[256,4224]{0,1:T(8,128)}), f32[256,4224]{0,1:T(8,128)}) %all-reduce.9.cloned.1.call-update) | async-done | bytes 4325392
  856.3 96.7 %all-gather.6.cloned.1.call-done = bf16[64,16,64,64]{3,2,1,0:T(8,128)(2,1)} async-done(((bf16[1,16,64,64]{3,2,1,0:T(8,128)(2,1)}), bf16[64,16,64,64]{3,2,1,0:T(8,128)(2,1)}) %all-gather.6.cloned.1.call-update) | async-done | bytes 8388624 | tf_op jit(solution)/shard_map/all_gather | solution.py:79
  953.0 16.5 reshape.306
  969.5 18.2 dot_general.73
  987.6 15.5 fusion
  1009.0 48.6 %all-gather.1 = bf16[64,4,1024]{2,1,0:T(4,128)(2,1)S(1)} all-gather(bf16[1,4,1024]{2,1,0:T(4,128)(2,1)S(1)} %fusion.64), channel_id=1, replica_groups=mesh['head'=4,'batch'=64] {'batch'}, dimensions={0}, use_global_device_ids=true | all-gather | bytes 532480 | tf_op jit(solution)/shard_map/all_gather | solution.py:145
  1058.2 13.7 psum.52
  1072.1 244.4 %psum.53 = f32[64,4]{1,0:T(8,128)S(1)} all-reduce(f32[64,4]{1,0:T(8,128)S(1)} %fusion.51), channel_id=1, replica_groups=mesh['head'=4,'batch'=64] {'batch'}, use_global_device_ids=true, to_apply=%region_10.11 | all-reduce | flops 256 | bytes 2048 | tf_op jit(solution)/shard_map/psum | solution.py:14
  1316.7 246.1 %psum.54 = f32[64,4]{1,0:T(8,128)S(1)} all-reduce(f32[64,4]{1,0:T(8,128)S(1)} %multiply_reduce_fusion), channel_id=1, replica_groups=mesh['head'=4,'batch'=64] {'batch'}, use_global_device_ids=true, to_apply=%region_12.13 | all-reduce | flops 256 | bytes 2048 | tf_op jit(solution)/shard_map/psum | solution.py:16
  1565.9 189.7 %all-reduce.11.cloned.1.call-done = f32[256,3584]{1,0:T(8,128)} async-done(((f32[256,3584]{1,0:T(8,128)}), f32[256,3584]{1,0:T(8,128)}) %all-reduce.11.cloned.1.call-update) | async-done | bytes 3670032
  1759.9 5.6 copy.153
  1769.9 67.1 %all-gather.8.cloned.1.call-done = bf16[64,4,3584]{2,1,0:T(4,128)(2,1)} async-done(((bf16[1,4,3584]{2,1,0:T(4,128)(2,1)}), bf16[64,4,3584]{2,1,0:T(4,128)(2,1)}) %all-gather.8.cloned.1.call-update) | async-done | bytes 1835024 | tf_op jit(solution)/shard_map/all_gather | solution.py:179
  1840.7 13.2 psum.55
  1853.9 123.7 %reduce-scatter.5.cloned.1.call-done = f32[64,256]{1,0:T(8,128)} async-done(((f32[4096,256]{1,0:T(8,128)}), f32[64,256]{1,0:T(8,128)}) %reduce-scatter.5.cloned.1.call-update) | async-done | bytes 65552 | tf_op jit(solution)/shard_map/reduce_scatter | solution.py:169
  (149 shorter events, 45.6 us)
Async XLA Ops:
  7.2 637.8 %copy-start = (bf16[4,64,1024]{2,1,0:T(8,128)(2,1)S(1)}, bf16[4,64,1024]{2,1,0:T(8,128)(2,1)}, u32[]{:S(2)}) copy-start(bf16[4,64,1024]{2,1,0:T(8,128)(2,1)} %param.32) | copy-start | bytes 1572868
  7.2 19.5 copy-start.15
  7.2 77.3 %copy-start.18 = (s32[1,4]{1,0:T(1,128)S(1)}, s32[1,4]{1,0:T(1,128)}, u32[]{:S(2)}) copy-start(s32[1,4]{1,0:T(1,128)} %param.23) | copy-start | bytes 52
  12.1 629.4 %all-to-all-start = ((bf16[2,1,4096]{0,1,2:T(2,128)(2,1)}), bf16[2,1,4096]{0,1,2:T(2,128)(2,1)S(1)}, u32[]{:S(2)}, u32[]{:S(2)}) async-start(bf16[2,1,4096]{0,1,2:T(2,128)(2,1)} %copy.119), calls=%async_computation | async-start | bytes 4194304 | tf_op jit(solution)/shard_map/all_to_all | solution.py:71
  25.3 823.8 %all-reduce.9.cloned.1.call-start = ((), (), s32[]{:S(2)}) async-start(), calls=%async_computation.5 | async-start | bytes 8650752
  132.9 508.5 %copy-start.16 = (f32[2,64]{1,0:T(2,128)S(1)}, f32[2,64]{1,0:T(2,128)}, u32[]{:S(2)}) copy-start(f32[2,64]{1,0:T(2,128)} %param.30) | copy-start | bytes 1540
  132.9 508.5 %copy-start.17 = (f32[2,64]{1,0:T(2,128)S(1)}, f32[2,64]{1,0:T(2,128)}, u32[]{:S(2)}) copy-start(f32[2,64]{1,0:T(2,128)} %param.29) | copy-start | bytes 1540
  132.9 511.8 %copy-start.9 = (f32[5,64]{1,0:T(8,128)S(1)}, f32[5,64]{1,0:T(8,128)}, u32[]{:S(2)}) copy-start(f32[5,64]{1,0:T(8,128)} %param.31) | copy-start | bytes 3844
  647.6 5.4 copy-start.8
  657.7 191.5 %copy-start.6 = (bf16[128,1024]{1,0:T(8,128)(2,1)S(1)}, bf16[128,1024]{1,0:T(8,128)(2,1)}, u32[]{:S(2)}) copy-start(bf16[128,1024]{1,0:T(8,128)(2,1)} %param.34) | copy-start | bytes 786436
  657.7 191.5 %copy-start.10 = (f32[1024]{0:T(1024)S(1)}, f32[1024]{0:T(1024)}, u32[]{:S(2)}) copy-start(f32[1024]{0:T(1024)} %param.35) | copy-start | bytes 12292
  657.7 295.3 %all-gather.6.cloned.1.call-start = ((), (), s32[]{:S(2)}) async-start(), calls=%async_computation.2 | async-start | bytes 17039360 | tf_op jit(solution)/shard_map/all_gather | solution.py:79
  658.4 1097.1 %all-reduce.11.cloned.1.call-start = ((), (), s32[]{:S(2)}) async-start(), calls=%async_computation.6 | async-start | bytes 7340032
  987.6 15.5 copy-start.2
  1003.2 5.8 copy-start.12
  1003.2 5.8 copy-start.13
  1003.7 54.1 %copy-start.7 = (bf16[64,1024]{1,0:T(8,128)(2,1)S(1)}, bf16[64,1024]{1,0:T(8,128)(2,1)}, u32[]{:S(2)}) copy-start(bf16[64,1024]{1,0:T(8,128)(2,1)} %param.39) | copy-start | bytes 393220
  1005.0 558.2 %copy-start.14 = (f32[2,64]{1,0:T(2,128)S(1)}, f32[2,64]{1,0:T(2,128)}, u32[]{:S(2)}) copy-start(f32[2,64]{1,0:T(2,128)} %param.40) | copy-start | bytes 1540
  1006.6 556.8 %copy-start.4 = (bf16[64,3584]{1,0:T(8,128)(2,1)S(1)}, bf16[64,3584]{1,0:T(8,128)(2,1)}, u32[]{:S(2)}) copy-start(bf16[64,3584]{1,0:T(8,128)(2,1)} %param.41) | copy-start | bytes 1376260
  1563.3 193.9 %copy-start.3 = (bf16[64,4096]{1,0:T(8,128)(2,1)S(1)}, bf16[64,4096]{1,0:T(8,128)(2,1)}, u32[]{:S(2)}) copy-start(bf16[64,4096]{1,0:T(8,128)(2,1)} %param.42) | copy-start | bytes 1572868
  1565.8 271.2 %all-gather.8.cloned.1.call-start = ((), (), s32[]{:S(2)}) async-start(), calls=%async_computation.3 | async-start | bytes 1863680 | tf_op jit(solution)/shard_map/all_gather | solution.py:179
  1757.1 220.5 %reduce-scatter.5.cloned.1.call-start = ((), (), s32[]{:S(2)}) async-start(), calls=%async_computation.4 | async-start | bytes 4259840 | tf_op jit(solution)/shard_map/reduce_scatter | solution.py:169
  1765.5 74.5 %copy-start.5 = (bf16[64,3584]{1,0:T(8,128)(2,1)S(1)}, bf16[64,3584]{1,0:T(8,128)(2,1)}, u32[]{:S(2)}) copy-start(bf16[64,3584]{1,0:T(8,128)(2,1)} %param.43) | copy-start | bytes 1376260
  1765.5 213.9 %copy-start.1 = (bf16[4,64,1024]{2,1,0:T(8,128)(2,1)S(1)}, bf16[4,64,1024]{2,1,0:T(8,128)(2,1)}, u32[]{:S(2)}) copy-start(bf16[4,64,1024]{2,1,0:T(8,128)(2,1)} %param.32) | copy-start | bytes 1572868
  (1 other events, 1.6 us)
Sparse Core Ops, SparseCore 0:
  657.8 191.2 all-reduce.8
  852.3 100.6 all-gather.5
  1566.0 189.5 all-reduce.10
  1759.1 77.9 all-gather.7
  1841.6 136.0 reduce-scatter.4
where the time goes:
time: 1990 us
  blocking collectives  1170 us (59%)
  waiting for transfers between devices  667 us (34%)
  local copies, waits for them, and re-layouts  76.2 us (4%)
  matrix products  30.9 us (2%)
    psum x2, blocking collectives, normalize(): lax.psum(jnp.sum(centered * centered, axis=-1), 'batch') / EMBEDDING_DIM  492 us
    psum x2, blocking collectives, normalize(): mean = lax.psum(jnp.sum(stream, axis=-1), 'batch') / EMBEDDING_DIM  489 us
    unnamed x7, waiting for transfers between devices  380 us
    reduce_scatter x1, waiting for transfers between devices, local(): lax.psum_scatter(lax.dot_general(part, mixed_two[1], (((0,), (1,)), ((),...  124 us
    all_gather x1, waiting for transfers between devices, local(): piece = lax.all_gather(memory_matrices, 'batch', axis=0, tiled=True)  96.7 us
    all_gather x1, waiting for transfers between devices, local(): lax.all_gather(units, 'batch', axis=0, tiled=True)  67.1 us
    unnamed x1, blocking collectives  55.7 us
    all_gather x1, blocking collectives, local(): lax.all_gather(gated, 'batch', axis=0, tiled=True)  48.6 us
  transfers between devices with their start and end apart: 6, of which 5 were waited for; matrix products, arithmetic and copies ran while one was open for 2% of the time, Pallas kernels for 0%

commit v1 on v0

v1 whole, which is shorter than its diff:
```python
import jax
import jax.numpy as jnp
from jax import lax
from jax.experimental import pallas as pl
from jax.experimental.pallas import tpu as pltpu
from jax.sharding import PartitionSpec as P

F32 = jnp.float32
BF16 = jnp.bfloat16
MESH = pl.DeviceIdType.MESH
EPS_LN = 1e-05
EPS_GN = 0.00064
NX, NY, NZ, NC = 4, 4, 8, 2
NQ = NY * NC
VM = pl.BlockSpec(memory_space=pltpu.VMEM)
ANY = pl.BlockSpec(memory_space=pl.ANY)
DMA = pltpu.SemaphoreType.DMA


def batch_of(y, z, c):
    return (y * NZ + z) * NC + c


def place():
    h = lax.axis_index("head")
    b = lax.axis_index("batch")
    c = lax.rem(b, NC)
    z = lax.rem(lax.div(b, NC), NZ)
    y = lax.div(b, NC * NZ)
    return h, b, y, z, c, y * NC + c


class Group:
    def __init__(self, kind):
        h, b, y, z, c, q = place()
        if kind == "z":
            self.me, self.n = z, NZ
            self.dev = lambda i: (h, batch_of(y, i, c))
        elif kind == "q":
            self.me, self.n = q, NQ
            self.dev = lambda i: (h, batch_of(lax.div(i, NC), z, lax.rem(i, NC)))
        elif kind == "x":
            self.me, self.n = h, NX
            self.dev = lambda i: (i, b)
        elif kind == "b":
            self.me, self.n = b, NY * NZ * NC
            self.dev = lambda i: (h, i)
        else:
            self.me, self.n = q * NX + h, NQ * NX

            def dev(i):
                k = lax.div(i, NX)
                return (lax.rem(i, NX), batch_of(lax.div(k, NC), z, lax.rem(k, NC)))

            self.dev = dev

    def each(self, body):
        def step(p, carry):
            body(p, lax.rem(self.me + p, self.n))
            return carry

        lax.fori_loop(1, self.n, step, 0)


def barrier(*groups):
    sem = pltpu.get_barrier_semaphore()
    for g in groups:
        g.each(
            lambda p, i: pl.semaphore_signal(
                sem, inc=1, device_id=g.dev(i), device_id_type=MESH
            )
        )
    pl.semaphore_wait(sem, sum(g.n - 1 for g in groups))


class Exchange:
    def __init__(self, group, src, dst, sems):
        self.g, self.src, self.dst, self.sems = group, src, dst, sems

    def copy(self, p, i):
        return pltpu.make_async_remote_copy(
            src_ref=self.src(i),
            dst_ref=self.dst(self.g.me),
            send_sem=self.sems.at[0, p],
            recv_sem=self.sems.at[1, p],
            device_id=self.g.dev(i),
            device_id_type=MESH,
        )

    def own(self):
        return pltpu.make_async_copy(
            self.src(self.g.me), self.dst(self.g.me), self.sems.at[0, 0]
        )

    def start(self):
        self.g.each(lambda p, i: self.copy(p, i).start())
        self.own().start()

    def arrive(self):
        self.own().wait()
        self.g.each(lambda p, i: self.copy(p, i).wait_recv())

    def drain(self):
        self.g.each(lambda p, i: self.copy(p, i).wait_send())

    @staticmethod
    def sem(n):
        return DMA((2, n))


def call(kernel, cid, outs, out_specs, in_specs, scratch, args):
    return pl.pallas_call(
        kernel,
        out_shape=[jax.ShapeDtypeStruct(s, d) for s, d in outs],
        in_specs=in_specs,
        out_specs=out_specs,
        scratch_shapes=scratch,
        compiler_params=pltpu.CompilerParams(collective_id=cid, has_side_effects=True),
        name="exchange_%d" % cid,
    )(*args)


def lanes(i, n):
    return pl.ds(pl.multiple_of(i, 128), n)


def chunk_start(i):
    return (7 * lax.div(i, 2) + 3 * lax.rem(i, 2)) * 128


def kernel_a(meta, state, params, low, maps, meta_o, state_o, params_o, low_o, maps_o, s0, s1, s2, s3, s4):
    gb, gq = Group("b"), Group("q")
    xs = [
        Exchange(gb, lambda i: meta, lambda m: meta_o.at[m], s0),
        Exchange(gq, lambda i: params, lambda m: params_o.at[m], s2),
        Exchange(gq, lambda i: low, lambda m: low_o.at[m], s3),
        Exchange(gq, lambda i: maps.at[:, :, lanes(i * 128, 128)], lambda m: maps_o.at[:, m], s4),
        Exchange(
            gb,
            lambda i: state.at[
                (lax.div(i, NC * NZ) * NC + lax.rem(i, NC)) * NZ + lax.rem(lax.div(i, NC), NZ)
            ],
            lambda m: state_o.at[m],
            s1,
        ),
    ]
    barrier(gb)
    for x in xs:
        x.start()
    for x in xs:
        x.arrive()
        x.drain()


def kernel_b(emb, edges, state, edges_o, state_o, stream_o, stats_o, xbuf, blk, st, s0, s1, s2, s3, s4):
    gb, gq, gx, gz = Group("b"), Group("q"), Group("x"), Group("z")
    ex = Exchange(gx, lambda i: emb, lambda m: xbuf.at[m], s0)
    ee = Exchange(
        gb, lambda i: edges.at[lax.rem(lax.div(i, NC), NZ)], lambda m: edges_o.at[m], s1
    )
    es = Exchange(gz, lambda i: state.at[i], lambda m: state_o.at[m], s2)
    barrier(gx, gb)
    ex.start()
    ee.start()
    es.start()
    ex.arrive()
    total = xbuf[0].astype(F32)
    for k in range(1, NX):
        total = total + xbuf[k].astype(F32)
    blk[...] = total.astype(BF16)
    mean = jnp.sum(total, axis=0, keepdims=True) * (1.0 / total.shape[0])
    dev = total - mean
    st[0:1, :] = mean
    st[1:2, :] = jnp.sum(dev * dev, axis=0, keepdims=True)
    eg = Exchange(gq, lambda i: blk, lambda m: stream_o.at[m], s3)
    et = Exchange(gb, lambda i: st, lambda m: stats_o.at[m], s4)
    eg.start()
    et.start()
    eg.arrive()
    et.arrive()
    ee.arrive()
    es.arrive()
    for x in (ex, ee, es, eg, et):
        x.drain()


def kernel_d(part, emit, look, acc, part_o, emit_o, look_o, acc_o, s0, s1, s2, s3):
    gq, gz = Group("q"), Group("z")
    h = lax.axis_index("head")
    xs = [
        Exchange(gz, lambda i: part.at[:, pl.ds(pl.multiple_of(i * 32, 32), 32)], lambda m: part_o.at[m], s0),
        Exchange(gq, lambda i: emit.at[:, lanes(i * 128, 128)], lambda m: emit_o.at[m], s1),
        Exchange(gq, lambda i: look.at[:, lanes(chunk_start(i), 512)], lambda m: look_o.at[m], s2),
        Exchange(
            gq,
            lambda i: acc.at[:, lanes((lax.div(i, NC) * NZ + 2 * h + lax.rem(i, NC)) * 128, 128)],
            lambda m: acc_o.at[m],
            s3,
        ),
    ]
    barrier(gz, gq)
    for x in xs:
        x.start()
    for x in xs:
        x.arrive()
        x.drain()


def kernel_e(gated, state, down, gated_o, state_o, down_o, s0, s1, s2):
    gq, gz = Group("q"), Group("z")
    xs = [
        Exchange(gz, lambda i: gated, lambda m: gated_o.at[m], s0),
        Exchange(gq, lambda i: state.at[i], lambda m: state_o.at[m], s1),
        Exchange(gq, lambda i: down.at[:, lanes(chunk_start(i), 512)], lambda m: down_o.at[m], s2),
    ]
    barrier(gz, gq)
    for x in xs:
        x.start()
    for x in xs:
        x.arrive()
        x.drain()


def kernel_f(part, stream, full_o, stats_o, rbuf, mine, st, s0, s1, s2):
    gg, gz = Group("g"), Group("z")
    er = Exchange(gg, lambda i: part.at[i], lambda m: rbuf.at[m], s0)
    barrier(gg, gz)
    er.start()
    er.arrive()
    mine[...] = stream[...] + jnp.sum(rbuf[...].astype(F32), axis=0)
    eg = Exchange(gg, lambda i: mine, lambda m: full_o.at[m], s1)
    eg.start()
    eg.arrive()
    n = gg.n * mine.shape[0]
    mean = jnp.sum(jnp.sum(full_o[...], axis=0), axis=0, keepdims=True) * (1.0 / n)
    dev = full_o[...] - mean[None]
    st[0:1, :] = mean
    st[1:2, :] = jnp.sum(jnp.sum(dev * dev, axis=0), axis=0, keepdims=True)
    es = Exchange(gz, lambda i: st, lambda m: stats_o.at[m], s2)
    es.start()
    es.arrive()
    for x in (er, eg, es):
        x.drain()


def kernel_i(part, rec, units_o, rec_o, rbuf, abuf, mine, sent, s0, s1, s2, s3):
    gz = Group("z")
    h, b, y, z, c, q = place()
    ep = Exchange(gz, lambda i: part.at[i], lambda m: rbuf.at[m], s0)
    ea = Exchange(gz, lambda i: rec.at[i], lambda m: abuf.at[m], s1)
    dest = (lax.rem(z, NX), batch_of(y, 2 * h + c, lax.div(z, NX)))
    source = (lax.div(z, 2), batch_of(y, c * NX + h, lax.rem(z, 2)))
    other = jnp.logical_or(dest[0] != h, dest[1] != b)

    def beyond(device):
        core = lax.rem(device[1], NC)
        return jnp.logical_or(device[0] != h, core != c)

    sem = pltpu.get_barrier_semaphore()
    gz.each(
        lambda p, i: pl.semaphore_signal(sem, inc=1, device_id=gz.dev(i), device_id_type=MESH)
    )

    @pl.when(beyond(source))
    def _():
        pl.semaphore_signal(sem, inc=1, device_id=source, device_id_type=MESH)

    pl.semaphore_wait(sem, gz.n - 1 + beyond(dest).astype(jnp.int32))

    ep.start()
    ea.start()
    ep.arrive()
    up = jnp.maximum(jnp.sum(rbuf[...].astype(F32), axis=0), 0.0)
    up = up * up
    lane = lax.broadcasted_iota(jnp.int32, up.shape, 1)
    mine[...] = jnp.where(jnp.logical_and(c == 1, lane < 128), 0.0, up).astype(BF16)
    eu = Exchange(gz, lambda i: mine, lambda m: units_o.at[m], s2)
    eu.start()
    ea.arrive()
    sent[...] = jax.nn.sigmoid(jnp.sum(abuf[...].astype(F32), axis=0))

    far = pltpu.make_async_remote_copy(
        src_ref=sent,
        dst_ref=rec_o,
        send_sem=s3.at[0],
        recv_sem=s3.at[1],
        device_id=dest,
        device_id_type=MESH,
    )

    @pl.when(other)
    def _():
        far.start()
        far.wait()

    @pl.when(jnp.logical_not(other))
    def _():
        near = pltpu.make_async_copy(sent, rec_o, s3.at[0])
        near.start()
        near.wait()

    eu.arrive()
    for x in (ep, ea, eu):
        x.drain()


def kernel_k(part, rec, stream, out, rbuf, mine, s0, s1):
    gg, gx = Group("g"), Group("x")
    er = Exchange(gg, lambda i: part.at[i], lambda m: rbuf.at[m], s0)
    barrier(gg)
    er.start()
    er.arrive()
    mine[...] = stream[...] + rec[...] * jnp.sum(rbuf[...].astype(F32), axis=0)
    eg = Exchange(gx, lambda i: mine, lambda m: out.at[m], s1)
    eg.start()
    eg.arrive()
    er.drain()
    eg.drain()


def join(stats, per, count):
    mean = jnp.mean(stats[:, 0], axis=0)
    spread = jnp.sum(stats[:, 1], axis=0) + per * jnp.sum(
        jnp.square(stats[:, 0] - mean[None]), axis=0
    )
    return mean, spread / count


def dot(a, b, ca, cb):
    return lax.dot_general(a, b, (((ca,), (cb,)), ((), ())), preferred_element_type=F32)


def local(
    query_symbol_numbers,
    alive_span_sizes,
    former_positions,
    previous_normed_vectors,
    memory_matrices,
    vocabulary_vectors,
    standardize_scales,
    standardize_shifts,
    timemix_blend_factors,
    timemix_linear_maps,
    forgetting_first_lowrank,
    forgetting_second_lowrank,
    forgetting_loglog_floor,
    current_reward_factor,
    perspan_standardize_scale,
    perspan_standardize_shift,
    timemix_emit_matrix,
    feedforward_blend_factors,
    feedforward_lookup_matrix,
    feedforward_accept_matrix,
    feedforward_emit_matrix,
):
    h, b, y, z, c, q = place()
    i32 = jnp.int32

    meta = jnp.concatenate(
        [query_symbol_numbers[0], alive_span_sizes, former_positions, jnp.zeros((122,), i32)]
    )[None]
    params = jnp.concatenate(
        [standardize_scales, standardize_shifts, timemix_blend_factors, feedforward_blend_factors]
    )
    params = jnp.pad(params, ((0, 5), (0, 64)))
    pieces = memory_matrices.reshape(64, 8, 128)
    S = Exchange.sem
    meta, pieces, params, low_w, maps = call(
        kernel_a,
        0,
        [
            ((64, 1, 128), i32),
            ((64, 8, 128), BF16),
            ((8, 16, 128), F32),
            ((8, 64, 128), BF16),
            ((4, 8, 64, 128), BF16),
        ],
        [VM, VM, VM, ANY, ANY],
        [VM, VM, VM, ANY, ANY],
        [S(64), S(64), S(8), S(8), S(8)],
        (meta, pieces, params, forgetting_first_lowrank, timemix_linear_maps),
    )
    meta = meta[:, 0]
    ids = meta[:, :4].reshape(NY, NZ, NC, 4).transpose(1, 3, 0, 2).reshape(256)
    lengths = meta[:, 4]
    owners = meta[:, 5].reshape(NY, NZ, NC).transpose(1, 0, 2).reshape(64)
    vocab_local = vocabulary_vectors.shape[1]
    offset = ids - h * vocab_local
    inside = (offset >= 0) & (offset < vocab_local)
    looked = jnp.take(vocabulary_vectors, jnp.clip(offset, 0, vocab_local - 1), axis=1)
    emb = jnp.where(inside[None], looked, jnp.zeros_like(looked))
    old = jnp.arange(64, dtype=i32)
    pick = owners[:, None] == old[None, :]
    pieces = dot(pick.astype(BF16), pieces.reshape(64, 1024), 1, 0).astype(BF16)
    params = params[:, :, :64].transpose(0, 2, 1).reshape(512, 16)
    scale, shift = params[:, 0:2], params[:, 2:4]
    mixes, mixes_two = params[:, 4:9], params[:, 9:11]

    edges = previous_normed_vectors.reshape(2, NY, NZ, 128).transpose(2, 0, 1, 3).reshape(NZ, 8, 128)
    edges, start, stream, stats = call(
        kernel_b,
        1,
        [((64, 8, 128), BF16), ((8, 8, 1024), BF16), ((8, 64, 256), BF16), ((64, 2, 256), F32)],
        [VM] * 4,
        [VM] * 3,
        [
            pltpu.VMEM((NX, 64, 256), BF16),
            pltpu.VMEM((64, 256), BF16),
            pltpu.VMEM((2, 256), F32),
            S(4),
            S(64),
            S(8),
            S(8),
            S(64),
        ],
        (emb, edges, pieces.reshape(8, 8, 1024)),
    )
    own_rows = lax.dynamic_slice(stream, (q, h * 16, 0), (1, 16, 256))[0].astype(F32)
    mean, var = join(stats, 64.0, 4096.0)
    tok_z = jnp.arange(256, dtype=i32) // 32
    tok_j = (jnp.arange(256, dtype=i32) // 8) % 4
    tok_q = jnp.arange(256, dtype=i32) % 8
    tok_r = (tok_q // 2 * 8 + tok_z) * 2 + tok_q % 2
    back = (
        (jnp.arange(256, dtype=i32)[:, None] + 8 == jnp.arange(256, dtype=i32)[None, :])
        & (tok_j[None, :] > 0)
    ).astype(BF16)
    owner_tok = jnp.broadcast_to(owners.reshape(8, 1, 8), (8, 4, 8)).reshape(256)
    first = ((old[:, None] == owner_tok[None, :]) & (tok_j[None, :] == 0)).astype(BF16)
    edges = edges.reshape(64, 2, 512)

    def normalize(x, mean, var, k):
        return (
            (x - mean[None]) * lax.rsqrt(var[None] + EPS_LN) * scale[:, k : k + 1]
            + shift[:, k : k + 1]
        ).astype(BF16)

    def shifted(normed, k, mixes):
        before = dot(normed, back, 1, 0) + dot(edges[:, k], first, 0, 0)
        now = normed.astype(F32)
        delta = before - now
        return [
            (now + delta * mixes[:, n : n + 1]).astype(BF16) for n in range(mixes.shape[1])
        ]

    normed = normalize(stream.reshape(512, 256).astype(F32), mean, var, 0)
    mixed = shifted(normed, 0, mixes)
    maps = maps.reshape(4, 512, 128)
    weights = [maps[n] for n in range(4)] + [low_w.reshape(512, 128)]
    part = jnp.stack([dot(m, w, 0, 0).astype(BF16) for m, w in zip(mixed, weights)])

    proj, emit, look, accept = call(
        kernel_d,
        2,
        [((8, 5, 32, 128), BF16), ((8, 64, 128), BF16), ((8, 64, 512), BF16), ((8, 64, 128), BF16)],
        [VM, ANY, ANY, ANY],
        [VM, ANY, ANY, ANY],
        [S(8)] * 4,
        (part, timemix_emit_matrix, feedforward_lookup_matrix, feedforward_accept_matrix),
    )
    proj = jnp.sum(proj.astype(F32), axis=0)
    low = jnp.tanh(proj[4]).astype(BF16)

    def mine(v):
        return lax.dynamic_slice_in_dim(v, q * 128, 128, v.ndim - 1)

    decay = jnp.exp(
        -jnp.exp(
            mine(forgetting_loglog_floor)[None]
            + jnp.dot(low, mine(forgetting_second_lowrank), preferred_element_type=F32)
        )
    )
    shape = (4, 8, 2, 64)
    rec, key, val = (proj[n].reshape(shape) for n in range(3))
    decay = decay.reshape(shape)
    bonus = mine(current_reward_factor).reshape(2, 64)
    lens_q = lax.dynamic_index_in_dim(lengths.reshape(NY, NZ, NC), z, 1, keepdims=False).reshape(8)
    state = (
        start.reshape(2, 4, 8, 16, 64).transpose(2, 0, 1, 3, 4).reshape(8, 2, 64, 64).astype(F32)
    )
    outs = []
    for j in range(4):
        r, k, v, d = rec[j], key[j], val[j], decay[j]
        within = jnp.sum(state * r[..., None], axis=2)
        within = within + jnp.sum(r * bonus[None] * k, axis=-1, keepdims=True) * v
        outs.append(within)
        alive = (j < lens_q)[:, None, None, None]
        state = jnp.where(alive, d[..., None] * state + k[..., None] * v[:, :, None, :], state)
    wkv = jnp.stack(outs)
    mu = jnp.mean(wkv, axis=-1, keepdims=True)
    spread = jnp.mean(jnp.square(wkv - mu), axis=-1, keepdims=True)
    grouped = ((wkv - mu) * lax.rsqrt(spread + EPS_GN)).reshape(32, 128)
    grouped = grouped * mine(perspan_standardize_scale)[None] + mine(perspan_standardize_shift)[None]
    gated = (grouped * jax.nn.silu(proj[3])).astype(BF16)

    gated, states, down = call(
        kernel_e,
        3,
        [((8, 32, 128), BF16), ((8, 64, 128), BF16), ((8, 64, 512), BF16)],
        [VM, VM, ANY],
        [VM, VM, ANY],
        [S(8)] * 3,
        (gated, state.astype(BF16).reshape(8, 64, 128), feedforward_emit_matrix),
    )
    new_states = states.reshape(1, 16, 64, 64)
    att = dot(emit.reshape(512, 128), gated.reshape(256, 128), 1, 1).astype(BF16)

    full, stats = call(
        kernel_f,
        4,
        [((32, 16, 256), F32), ((8, 2, 256), F32)],
        [VM] * 2,
        [VM] * 2,
        [
            pltpu.VMEM((32, 16, 256), BF16),
            pltpu.VMEM((16, 256), F32),
            pltpu.VMEM((2, 256), F32),
            S(32),
            S(32),
            S(8),
        ],
        (att.reshape(32, 16, 256), own_rows),
    )
    own_two = lax.dynamic_index_in_dim(full, q * 4 + h, 0, keepdims=False)
    mean, var = join(stats, 512.0, 4096.0)
    normed_two = normalize(full.reshape(512, 256), mean, var, 1)
    mixed_two = shifted(normed_two, 1, mixes_two)
    part = dot(mixed_two[0], look.reshape(512, 512), 0, 0).astype(BF16).reshape(8, 32, 512)
    recv = dot(accept.reshape(512, 128), mixed_two[1], 0, 0).astype(BF16).reshape(8, 16, 256)

    units, recv = call(
        kernel_i,
        5,
        [((8, 32, 512), BF16), ((16, 256), F32)],
        [VM] * 2,
        [VM] * 2,
        [
            pltpu.VMEM((8, 32, 512), BF16),
            pltpu.VMEM((8, 16, 256), BF16),
            pltpu.VMEM((32, 512), BF16),
            pltpu.VMEM((16, 256), F32),
            S(8),
            S(8),
            S(8),
            DMA((2,)),
        ],
        (part, recv),
    )
    values = dot(down.reshape(512, 512), units.reshape(256, 512), 1, 1).astype(BF16)

    (result,) = call(
        kernel_k,
        6,
        [((4, 16, 256), F32)],
        [VM],
        [VM] * 3,
        [pltpu.VMEM((32, 16, 256), BF16), pltpu.VMEM((16, 256), F32), S(32), S(4)],
        (values.reshape(32, 16, 256), recv, own_two),
    )
    result = result.reshape(64, NZ, 4, NY, NC).transpose(3, 1, 4, 2, 0).reshape(64, 4, 64)
    live = jnp.arange(4, dtype=i32)[None, :] < lengths[:, None]
    hidden = jnp.where(live[..., None], result, jnp.float32(0.0))
    last = ((tok_r[:, None] == old[None, :]) & (tok_j[:, None] == lengths[None, :] - 1)).astype(BF16)

    def last_of(normed):
        rows = lax.dynamic_slice_in_dim(normed, q * 64, 64, 0)
        return dot(last, rows, 0, 1).astype(BF16)

    new_edges = jnp.stack([last_of(normed), last_of(normed_two)])
    return (hidden, new_edges, new_states)


def solution(mesh):
    return jax.shard_map(
        local,
        mesh=mesh,
        in_specs=(
            P("batch", None),
            P("batch"),
            P("batch"),
            P(None, "batch", None),
            P("batch", "head", None, None),
            P("batch", "head"),
            P(None, "batch"),
            P(None, "batch"),
            P(None, "batch"),
            P(None, "batch", "head"),
            P("batch", None),
            P(None, "head"),
            P("head"),
            P("head"),
            P("head"),
            P("head"),
            P("batch", "head"),
            P(None, "batch"),
            P("batch", "head"),
            P("batch", None),
            P("batch", "head"),
        ),
        out_specs=(P(None, None, "batch"), P(None, None, "batch"), P("batch", "head", None, None)),
        check_vma=False,
    )
```

time: 1990 us -> 217 us (0.11)
  blocking collectives: 1170 us -> 0 us
  waiting for transfers between devices: 667 us -> 0 us
  Pallas kernels: 0 us -> 147 us
  local copies, waits for them, and re-layouts: 76.2 us -> 32 us
    psum x7 -> x0, blocking collectives: 1020 us -> none  [the longest x2 492 us: normalize(): lax.psum(jnp.sum(centered * centered, axis=-1), 'batch') / EMBEDDING_DIM]
    unnamed x7 -> x0, waiting for transfers between devices: 380 us -> none
    all_gather x2 -> x0, waiting for transfers between devices: 164 us -> none  [the longest x1 96.7 us: local(): piece = lax.all_gather(memory_matrices, 'batch', axis=0, tiled=True)]
    pallas_call x0 -> x7, Pallas kernels: none -> 147 us  [call(): pl.pallas_call(kernel, out_shape=[jax.ShapeDtypeStruct(s, d) for s, d in...]
    reduce_scatter x1 -> x0, waiting for transfers between devices: 124 us -> none  [local(): lax.psum_scatter(lax.dot_general(part, mixed_two[1], (((0,), (1,)), ((),...]
    all_gather x2 -> x0, blocking collectives: 91.7 us -> none  [the longest x1 48.6 us: local(): lax.all_gather(gated, 'batch', axis=0, tiled=True)]
    unnamed x1 -> x0, blocking collectives: 55.7 us -> none
  transfers between devices with their start and end apart: 6 -> 0, of which waited for: 5 -> 0; matrix products, arithmetic and copies ran while one was open for 2% -> 0% of each run, Pallas kernels for 0% -> 0%
where the time goes in v1:
time: 217 us; the launch traced here: 215 us
  Pallas kernels  147 us (68%)
  local copies, waits for them, and re-layouts  32 us (15%)
  other arithmetic  18.5 us (9%)
  matrix products  14.3 us (7%)
  between operations  2.95 us (1%)
    pallas_call x7, Pallas kernels, call(): pl.pallas_call(kernel, out_shape=[jax.ShapeDtypeStruct(s, d) for s, d in...  147 us
    dot_general x16, matrix products, dot(): lax.dot_general(a, b, (((ca,), (cb,)), ((), ())), preferred_element_type=...  14.1 us
    unnamed x43, local copies, waits for them, and re-layouts  5.45 us

profile of v1, /device:TPU:1, one launch (start us, length us, event | category | flops | bytes accessed | tf_op | source)
XLA Modules:
  0.0 215.2 jit_solution(14853618217008077095)
XLA Ops:
  5.3 1.2 add_bitcast_fusion.meta
  6.5 1.3 select_maximum_fusion.params
  9.2 1.8 reshape.591.state
  11.0 28.4 %exchange_0.1 = (s32[64,1,128]{2,1,0:T(1,128)}, bf16[64,8,128]{2,1,0:T(8,128)(2,1)}, f32[8,16,128]{2,1,0:T(8,128)}, bf16[8,64,128]{2,1,0:T(8,128)(2,1)}, bf16[4,8,64,128]{3,2,1,0:T(8,128)(2,1)}) custom-call(s32[1,128]{1,0:T(1,128)} %add_bitcast_fusion.meta, bf16[64,8,128]{2,1,0:T(8,128)(2,1)} %reshape.591.state, f32[16,128]{1,0:T(8,128)} %select_maximum_fusion.params, ...), custom_call_target="tpu_custom_call" | custom-call | tf_op jit(solution)/shard_map/exchange_0/pallas_call | solution.py:112
  44.4 1.8 fusion.2.state
  48.6 1.1 fusion.98
  49.7 3.2 %copy.66 = bf16[64,16384]{0,1:T(8,128)(2,1)} copy(bf16[64,16384]{1,0:T(8,128)(2,1)S(1)} %copy-done.1) | data formatting | bytes 4194304 | tf_op args[5]
  52.9 3.5 %gather_fusion = bf16[256,64]{1,0:T(8,128)(2,1)S(1)} fusion(bf16[64,16384]{0,1:T(8,128)(2,1)} %copy.66, s32[1024]{0:T(1024)S(1)} %pad_clamp_fusion), kind=kCustom, calls=%fused_computation | custom fusion | bytes 66560 | tf_op jit(solution)/shard_map/jit(_take)/gather | solution.py:390
  57.1 23.4 %exchange_1.1 = (bf16[64,8,128]{2,1,0:T(8,128)(2,1)}, bf16[8,8,1024]{2,1,0:T(8,128)(2,1)}, bf16[8,64,256]{2,1,0:T(8,128)(2,1)}, f32[64,2,256]{2,1,0:T(2,128)}) custom-call(bf16[64,256]{1,0:T(8,128)(2,1)} %select_bitcast_fusion.emb, bf16[8,8,128]{2,1,0:T(8,128)(2,1)} %bitcast.212, bf16[8,8,1024]{2,1,0:T(8,128)(2,1)} %fusion.2.state), custom_call_target="tpu_custom_call" | custom-call | tf_op jit(solution)/shard_map/exchange_1/pallas_call | solution.py:112
  80.5 1.3 bitcast_convert_fusion.stream
  83.0 1.2 fusion.28
  90.3 15.7 %exchange_2.1 = (bf16[8,5,32,128]{3,2,1,0:T(8,128)(2,1)}, bf16[8,64,128]{2,1,0:T(8,128)(2,1)}, bf16[8,64,512]{2,1,0:T(8,128)(2,1)}, bf16[8,64,128]{2,1,0:T(8,128)(2,1)}) custom-call(bf16[5,256,128]{2,1,0:T(8,128)(2,1)} %copy-done.4, bf16[64,1024]{1,0:T(8,128)(2,1)} %emit.1, bf16[64,3584]{1,0:T(8,128)(2,1)} %look.1, bf16[64,4096]{1,0:T(8,128)(2,1)} %acc.1), custom_call_target="tpu_custom_call" | custom-call | tf_op jit(solution)/shard_map/exchange_2/pallas_call | solution.py:112
  109.8 1.8 multiply_reduce_fusion.1
  115.9 1.6 select_convert_fusion.state
  117.5 14.8 %exchange_3.1 = (bf16[8,32,128]{2,1,0:T(8,128)(2,1)}, bf16[8,64,128]{2,1,0:T(8,128)(2,1)}, bf16[8,64,512]{2,1,0:T(8,128)(2,1)}) custom-call(bf16[32,128]{1,0:T(8,128)(2,1)} %multiply_convert_fusion.gated, bf16[8,64,128]{2,1,0:T(8,128)(2,1)} %select_convert_fusion.state, bf16[64,3584]{1,0:T(8,128)(2,1)} %down.1), custom_call_target="tpu_custom_call" | custom-call | tf_op jit(solution)/shard_map/exchange_3/pallas_call | solution.py:112
  132.4 1.8 convolution_convert_fusion.2
  134.2 1.7 reshape.612
  136.0 25.9 %exchange_4.1 = (f32[32,16,256]{2,1,0:T(8,128)}, f32[8,2,256]{2,1,0:T(2,128)}) custom-call(bf16[32,16,256]{2,1,0:T(8,128)(2,1)} %bitcast.184, f32[16,256]{1,0:T(8,128)} %bitcast_convert_fusion.stream), custom_call_target="tpu_custom_call" | custom-call | tf_op jit(solution)/shard_map/exchange_4/pallas_call | solution.py:112
  162.8 1.3 dynamic-slice_bitcast_fusion.stream
  164.1 1.2 fusion.32
  168.9 1.8 convolution_convert_fusion.1
  171.7 21.7 %exchange_5.1 = (bf16[8,32,512]{2,1,0:T(8,128)(2,1)}, f32[16,256]{1,0:T(8,128)}) custom-call(bf16[8,32,512]{2,1,0:T(8,128)(2,1)} %bitcast.185, bf16[8,16,256]{2,1,0:T(8,128)(2,1)} %bitcast.201), custom_call_target="tpu_custom_call" | custom-call | tf_op jit(solution)/shard_map/exchange_5/pallas_call | solution.py:112
  193.4 2.0 convolution_convert_fusion
  195.4 17.4 %exchange_6.1 = f32[4,16,256]{2,1,0:T(8,128)} custom-call(bf16[32,16,256]{2,1,0:T(8,128)(2,1)} %bitcast.186, f32[16,256]{1,0:T(8,128)} %get-tuple-element.41.rec, f32[16,256]{1,0:T(8,128)} %dynamic-slice_bitcast_fusion.stream), custom_call_target="tpu_custom_call" | custom-call | tf_op jit(solution)/shard_map/exchange_6/pallas_call | solution.py:112
  (178 shorter events, 35.1 us)
Async XLA Ops:
  0.6 106.4 %copy-start = (bf16[128,1024]{1,0:T(8,128)(2,1)S(1)}, bf16[128,1024]{1,0:T(8,128)(2,1)}, u32[]{:S(2)}) copy-start(bf16[128,1024]{1,0:T(8,128)(2,1)} %param.32) | copy-start | bytes 786436
  0.6 49.1 %copy-start.1 = (bf16[64,16384]{1,0:T(8,128)(2,1)S(1)}, bf16[64,16384]{1,0:T(8,128)(2,1)}, u32[]{:S(2)}) copy-start(bf16[64,16384]{1,0:T(8,128)(2,1)} %param.26) | copy-start | bytes 6291460
  2.2 85.1 %copy-start.12 = (pred[256]{0:T(512)(128)(4,1)}, pred[256]{0:T(512)(128)(4,1)S(1)}, u32[]{:S(2)}) copy-start(pred[256]{0:T(512)(128)(4,1)S(1)} %broadcast_compare_fusion.1) | copy-start | bytes 772
  6.5 80.4 %copy-start.11 = (s32[256]{0:T(256)}, s32[256]{0:T(256)S(1)}, u32[]{:S(2)}) copy-start(s32[256]{0:T(256)S(1)} %iota_add_fusion) | copy-start | bytes 3076
  6.5 77.6 %copy-start.16 = (s32[256]{0:T(256)}, s32[256]{0:T(256)S(1)}, u32[]{:S(2)}) copy-start(s32[256]{0:T(256)S(1)} %get-tuple-element.104) | copy-start | bytes 3076
  6.5 77.6 %copy-start.17 = (s32[256]{0:T(256)}, s32[256]{0:T(256)S(1)}, u32[]{:S(2)}) copy-start(s32[256]{0:T(256)S(1)} %get-tuple-element.105) | copy-start | bytes 3076
  40.5 43.6 %copy-start.19 = (s32[64]{0:T(128)}, s32[64]{0:T(128)S(1)}, u32[]{:S(2)}) copy-start(s32[64]{0:T(128)S(1)} %broadcast_add_fusion) | copy-start | bytes 772
  43.9 65.9 %copy-start.13 = (pred[8]{0:T(512)(128)(4,1)}, pred[8]{0:T(512)(128)(4,1)S(1)}, u32[]{:S(2)}) copy-start(pred[8]{0:T(512)(128)(4,1)S(1)} %gt.54) | copy-start | bytes 28
  44.0 65.8 %copy-start.14 = (pred[8]{0:T(512)(128)(4,1)}, pred[8]{0:T(512)(128)(4,1)S(1)}, u32[]{:S(2)}) copy-start(pred[8]{0:T(512)(128)(4,1)S(1)} %gt.56) | copy-start | bytes 28
  44.1 65.8 %copy-start.15 = (pred[8]{0:T(512)(128)(4,1)}, pred[8]{0:T(512)(128)(4,1)S(1)}, u32[]{:S(2)}) copy-start(pred[8]{0:T(512)(128)(4,1)S(1)} %gt.52) | copy-start | bytes 28
  46.4 40.9 %copy-start.8 = (s32[256]{0:T(256)}, s32[256]{0:T(256)S(1)}, u32[]{:S(2)}) copy-start(s32[256]{0:T(256)S(1)} %eq.95) | copy-start | bytes 3076
  47.0 39.9 %copy-start.10 = (pred[256]{0:T(512)(128)(4,1)}, pred[256]{0:T(512)(128)(4,1)S(1)}, u32[]{:S(2)}) copy-start(pred[256]{0:T(512)(128)(4,1)S(1)} %get-tuple-element.107) | copy-start | bytes 772
  85.6 3.5 %copy-start.7 = (bf16[8,64,128]{2,1,0:T(8,128)(2,1)S(1)}, bf16[8,64,128]{2,1,0:T(8,128)(2,1)}, u32[]{:S(2)}) copy-start(bf16[8,64,128]{2,1,0:T(8,128)(2,1)} %get-tuple-element.31) | copy-start | bytes 393220
  89.6 0.7 copy-start.4
  114.5 17.9 %copy-start.6 = (bf16[8,64,128]{2,1,0:T(8,128)(2,1)S(1)}, bf16[8,64,128]{2,1,0:T(8,128)(2,1)}, u32[]{:S(2)}) copy-start(bf16[8,64,128]{2,1,0:T(8,128)(2,1)} %get-tuple-element.34) | copy-start | bytes 393220
  115.9 53.1 %copy-start.2 = (bf16[8,64,512]{2,1,0:T(8,128)(2,1)S(1)}, bf16[8,64,512]{2,1,0:T(8,128)(2,1)}, u32[]{:S(2)}) copy-start(bf16[8,64,512]{2,1,0:T(8,128)(2,1)} %get-tuple-element.38) | copy-start | bytes 1572868
  115.9 54.9 %copy-start.5 = (bf16[8,64,128]{2,1,0:T(8,128)(2,1)S(1)}, bf16[8,64,128]{2,1,0:T(8,128)(2,1)}, u32[]{:S(2)}) copy-start(bf16[8,64,128]{2,1,0:T(8,128)(2,1)} %get-tuple-element.39) | copy-start | bytes 393220
  117.5 53.2 %copy-start.9 = (f32[512,1]{0,1:T(1,128)S(1)}, f32[512,1]{0,1:T(1,128)}, u32[]{:S(2)}) copy-start(f32[512,1]{0,1:T(1,128)} %get-tuple-element.88) | copy-start | bytes 6148
  132.4 61.1 %copy-start.3 = (bf16[8,64,512]{2,1,0:T(8,128)(2,1)S(1)}, bf16[8,64,512]{2,1,0:T(8,128)(2,1)}, u32[]{:S(2)}) copy-start(bf16[8,64,512]{2,1,0:T(8,128)(2,1)} %get-tuple-element.33) | copy-start | bytes 1572868
  165.4 49.0 %copy-start.18 = (pred[64,4]{0,1:T(4,128)(4,1)S(1)}, pred[64,4]{0,1:T(4,128)(4,1)}, u32[]{:S(2)}) copy-start(pred[64,4]{0,1:T(4,128)(4,1)} %iota_compare_fusion.7) | copy-start | bytes 772

commit v2 on v0

v2 whole, which is shorter than its diff:
```python
import jax
import jax.numpy as jnp
from jax import lax
from jax.experimental import pallas as pl
from jax.experimental.pallas import tpu as pltpu
from jax.sharding import PartitionSpec as P

F32 = jnp.float32
BF16 = jnp.bfloat16
MESH = pl.DeviceIdType.MESH
EPS_LN = 1e-05
EPS_GN = 0.00064
NX, NY, NZ, NC = 4, 4, 8, 2
NQ = NY * NC
VM = pl.BlockSpec(memory_space=pltpu.VMEM)
ANY = pl.BlockSpec(memory_space=pl.ANY)
DMA = pltpu.SemaphoreType.DMA


def batch_of(y, z, c):
    return (y * NZ + z) * NC + c


def place():
    h = lax.axis_index("head")
    b = lax.axis_index("batch")
    c = lax.rem(b, NC)
    z = lax.rem(lax.div(b, NC), NZ)
    y = lax.div(b, NC * NZ)
    return h, b, y, z, c, y * NC + c


class Group:
    def __init__(self, kind):
        h, b, y, z, c, q = place()
        if kind == "z":
            self.me, self.n = z, NZ
            self.dev = lambda i: (h, batch_of(y, i, c))
        elif kind == "q":
            self.me, self.n = q, NQ
            self.dev = lambda i: (h, batch_of(lax.div(i, NC), z, lax.rem(i, NC)))
        elif kind == "x":
            self.me, self.n = h, NX
            self.dev = lambda i: (i, b)
        elif kind == "b":
            self.me, self.n = b, NY * NZ * NC
            self.dev = lambda i: (h, i)
        else:
            self.me, self.n = q * NX + h, NQ * NX

            def dev(i):
                k = lax.div(i, NX)
                return (lax.rem(i, NX), batch_of(lax.div(k, NC), z, lax.rem(k, NC)))

            self.dev = dev

    def each(self, body):
        def step(p, carry):
            body(p, lax.rem(self.me + p, self.n))
            return carry

        lax.fori_loop(1, self.n, step, 0)


def barrier(*groups):
    sem = pltpu.get_barrier_semaphore()
    for g in groups:
        g.each(
            lambda p, i: pl.semaphore_signal(
                sem, inc=1, device_id=g.dev(i), device_id_type=MESH
            )
        )
    pl.semaphore_wait(sem, sum(g.n - 1 for g in groups))


class Exchange:
    def __init__(self, group, src, dst, whole, sems):
        self.g, self.src, self.dst, self.whole, self.sems = group, src, dst, whole, sems

    def copy(self, i):
        return pltpu.make_async_remote_copy(
            src_ref=self.src(i),
            dst_ref=self.dst(self.g.me),
            send_sem=self.sems.at[0],
            recv_sem=self.sems.at[1],
            device_id=self.g.dev(i),
            device_id_type=MESH,
        )

    def start(self):
        self.g.each(lambda p, i: self.copy(i).start())
        pltpu.make_async_copy(self.src(self.g.me), self.dst(self.g.me), self.sems.at[1]).start()

    def arrive(self):
        pltpu.make_async_copy(self.whole, self.whole, self.sems.at[1]).wait()

    def drain(self):
        part = self.dst(0)
        for _ in range(1):
            self.g.each(
                lambda p, i: pltpu.make_async_copy(part, part, self.sems.at[0]).wait()
            )


def lanes(i, n):
    return pl.ds(pl.multiple_of(i, 128), n)


def rows(i, n):
    return pl.ds(pl.multiple_of(i, n), n)


def chunk_start(i):
    return (7 * lax.div(i, 2) + 3 * lax.rem(i, 2)) * 128


def iota(shape, axis):
    return lax.broadcasted_iota(jnp.int32, shape, axis)


def dot(a, b, cb=0):
    return lax.dot_general(a, b, (((1,), (cb,)), ((), ())), preferred_element_type=F32)


def head_sum(x):
    left = iota(x.shape, 1) < 64
    a = jnp.sum(jnp.where(left, x, 0.0), axis=1, keepdims=True)
    b = jnp.sum(jnp.where(left, 0.0, x), axis=1, keepdims=True)
    return jnp.where(left, a, b)


def split(x):
    high = x.astype(BF16)
    return high, (x - high.astype(F32)).astype(BF16)


def join(stats, per, count):
    blocks = stats[...]
    total = jnp.sum(blocks, axis=0)
    mean = total[0:1] * (1.0 / blocks.shape[0])
    dev = blocks - mean[None]
    between = jnp.sum(dev * dev, axis=0)[0:1]
    return mean, (total[1:2] + per * between) * (1.0 / count)


def block_stats(x, st):
    mean = jnp.sum(x, axis=0, keepdims=True) * (1.0 / x.shape[0])
    dev = x - mean
    st[0:1, :] = mean
    st[1:2, :] = jnp.sum(dev * dev, axis=0, keepdims=True)
    return dev


INPUTS = [
    "ids", "lens", "pos", "gains", "biases", "mixes", "mixes2", "edges", "state", "low", "maps",
    "emit", "look", "acc", "down", "vocab", "second", "floor", "bonus", "gn_gain", "gn_bias",
]
SPACES = ["S"] * 3 + ["V"] * 6 + ["A"] * 7 + ["V"] * 5
OUTPUTS = ["hidden", "new_edges", "states"]
SCRATCH = [
    ("meta_s", (1, 128), jnp.int32),
    ("meta_r", (64, 1, 128), jnp.int32),
    ("prm_s", (16, 128), F32),
    ("prm_r", (8, 16, 128), F32),
    ("edges_r", (64, 8, 128), BF16),
    ("edges_f", (64, 8, 128), F32),
    ("state_r", (64, 8, 128), BF16),
    ("state_s", (64, 8, 128), BF16),
    ("state_z", (8, 8, 8, 128), BF16),
    ("low_w", (8, 64, 128), BF16),
    ("maps_w", (4, 8, 64, 128), BF16),
    ("emit_w", (8, 64, 128), BF16),
    ("look_w", (8, 64, 512), BF16),
    ("acc_w", (8, 64, 128), BF16),
    ("down_w", (8, 64, 512), BF16),
    ("vocab_w", (64, 16384), BF16),
    ("table", (64, 128), F32),
    ("emb_s", (64, 256), BF16),
    ("emb_r", (NX, 64, 256), BF16),
    ("blk", (64, 256), BF16),
    ("st", (2, 256), F32),
    ("st_r", (64, 2, 256), F32),
    ("stream_r", (8, 64, 256), BF16),
    ("part_s", (5, 256, 128), BF16),
    ("part_r", (8, 5, 32, 128), BF16),
    ("bd", (8, 128, 128), BF16),
    ("gated_s", (32, 128), BF16),
    ("gated_r", (8, 32, 128), BF16),
    ("new_s", (8, 64, 128), BF16),
    ("att_s", (8, 64, 256), BF16),
    ("att_r", (8, 64, 256), BF16),
    ("attx_s", (64, 256), BF16),
    ("attx_r", (NX, 64, 256), BF16),
    ("two", (64, 256), F32),
    ("dev_s", (64, 256), BF16),
    ("st2", (2, 256), F32),
    ("st2_r", (64, 2, 256), F32),
    ("dev_r", (8, 64, 256), BF16),
    ("up_s", (8, 32, 512), BF16),
    ("up_r", (8, 32, 512), BF16),
    ("rec_s", (8, 16, 256), BF16),
    ("rec_r", (8, 16, 256), BF16),
    ("units_s", (32, 512), BF16),
    ("units_r", (8, 32, 512), BF16),
    ("sig_s", (16, 256), F32),
    ("sig_r", (4, 16, 256), F32),
    ("val_s", (8, 64, 256), BF16),
    ("val_r", (8, 64, 256), BF16),
    ("valx_s", (64, 256), BF16),
    ("valx_r", (NX, 64, 256), BF16),
    ("norm_t", (512, 256), F32),
]
SEMS = [
    "meta", "prm", "edges", "state", "zstate", "low", "maps", "emit", "look", "acc", "down", "emb",
    "stats", "stream", "part", "gated", "new", "att", "attx", "stats2", "dev2", "up", "rec",
    "units", "val", "valx",
]


class Refs:
    pass


def kernel(*refs):
    r, s = Refs(), Refs()
    names = INPUTS + OUTPUTS + [n for n, _, _ in SCRATCH]
    for name, ref in zip(names, refs):
        setattr(r, name + ("_o" if name in OUTPUTS else ""), ref)
    for name, ref in zip(SEMS + ["sig", "vocab", "smem"], refs[len(names) :]):
        setattr(s, name, ref)
    meta_m = refs[-1]
    h, b, y, z, c, q = place()
    gb, gq, gx, gz = Group("b"), Group("q"), Group("x"), Group("z")

    dest = lambda k: (k, batch_of(y, 2 * h + c, lax.div(z, NX)))
    source = lambda k: (lax.div(z, 2), batch_of(y, c * NX + k, lax.rem(z, 2)))
    dest_here = dest(0)[1] == b

    sem = pltpu.get_barrier_semaphore()
    for g in (gb, gx):
        g.each(
            lambda p, i: pl.semaphore_signal(sem, inc=1, device_id=g.dev(i), device_id_type=MESH)
        )
    for k in range(4):
        far = source(k)

        @pl.when(jnp.logical_and(far[0] != h, far[1] != b))
        def _():
            pl.semaphore_signal(sem, inc=1, device_id=far, device_id_type=MESH)

    vocab_in = pltpu.make_async_copy(r.vocab, r.vocab_w, s.vocab)
    vocab_in.start()
    lane = iota((1, 128), 1)
    meta = jnp.where(lane == 4, r.lens[0], jnp.where(lane == 5, r.pos[0], 0))
    for j in range(4):
        meta = jnp.where(lane == j, r.ids[0, j], meta)
    r.meta_s[...] = meta
    r.prm_s[...] = jnp.zeros((16, 128), F32)
    r.prm_s[0:2, 0:64] = r.gains[...]
    r.prm_s[2:4, 0:64] = r.biases[...]
    r.prm_s[4:9, 0:64] = r.mixes[...]
    r.prm_s[9:11, 0:64] = r.mixes2[...]
    prm = r.prm_s[...]
    r.prm_s[...] = jnp.where(c == 0, prm, pltpu.roll(prm, 64, 1))

    pl.semaphore_wait(sem, gb.n - 1 + gx.n - 1 + 3 * (1 - dest_here.astype(jnp.int32)))

    def same(ref):
        return lambda i: ref

    def slots(ref):
        return lambda m: ref.at[m]

    x_meta = Exchange(gb, same(r.meta_s), slots(r.meta_r), r.meta_r, s.meta)
    x_prm = Exchange(gq, same(r.prm_s), slots(r.prm_r), r.prm_r, s.prm)
    x_edges = Exchange(
        gb, lambda i: r.edges.at[lax.rem(lax.div(i, NC), NZ)], slots(r.edges_r), r.edges_r, s.edges
    )
    x_state = Exchange(
        gb,
        lambda i: r.state.at[
            (lax.div(i, NC * NZ) * NC + lax.rem(i, NC)) * NZ + lax.rem(lax.div(i, NC), NZ)
        ],
        slots(r.state_r),
        r.state_r,
        s.state,
    )
    x_low = Exchange(gq, same(r.low), slots(r.low_w), r.low_w, s.low)
    x_maps = Exchange(
        gq,
        lambda i: r.maps.at[:, :, lanes(i * 128, 128)],
        lambda m: r.maps_w.at[:, m],
        r.maps_w,
        s.maps,
    )
    x_emit = Exchange(gq, lambda i: r.emit.at[:, lanes(i * 128, 128)], slots(r.emit_w), r.emit_w, s.emit)
    x_look = Exchange(
        gq, lambda i: r.look.at[:, lanes(chunk_start(i), 512)], slots(r.look_w), r.look_w, s.look
    )
    x_acc = Exchange(
        gq,
        lambda i: r.acc.at[:, lanes((lax.div(i, NC) * NZ + 2 * h + lax.rem(i, NC)) * 128, 128)],
        slots(r.acc_w),
        r.acc_w,
        s.acc,
    )
    x_down = Exchange(
        gq, lambda i: r.down.at[:, lanes(chunk_start(i), 512)], slots(r.down_w), r.down_w, s.down
    )
    for x in (x_meta, x_prm, x_edges, x_state, x_maps, x_low, x_emit, x_look, x_acc, x_down):
        x.start()

    x_meta.arrive()
    to_smem = pltpu.make_async_copy(r.meta_r, meta_m, s.smem)
    to_smem.start()
    meta = r.meta_r[...].reshape(64, 128)
    high = lax.shift_right_logical(meta, 8)
    lowb = (meta - high * 256).astype(F32).astype(BF16)
    high = high.astype(F32).astype(BF16)

    def device_of(zz, qq):
        return (lax.shift_right_logical(qq, 1) * NZ + zz) * NC + (qq & 1)

    tok = iota((256, 64), 0)
    by_tok = device_of(lax.shift_right_logical(tok, 5), tok & 7) == iota((256, 64), 1)
    by_tok = jnp.where(by_tok, 1.0, 0.0).astype(BF16)
    cols = dot(by_tok, high) * 256.0 + dot(by_tok, lowb)
    req = iota((64, 64), 0)
    by_req = device_of(lax.shift_right_logical(req, 3), req & 7) == iota((64, 64), 1)
    by_req = jnp.where(by_req, 1.0, 0.0).astype(BF16)
    r.table[...] = dot(by_req, lowb)
    tok_rows = cols.T
    lane_t = iota((1, 256), 1)
    slot = lax.shift_right_logical(lane_t, 3) & 3
    ids = tok_rows[0:1]
    for j in range(1, 4):
        ids = jnp.where(slot == j, tok_rows[j : j + 1], ids)
    ids = ids.astype(jnp.int32) - h * 16384
    length = tok_rows[4:5].astype(jnp.int32)

    vocab_in.wait()
    step = 1024

    def look_up(k, acc):
        base = pl.multiple_of(k * step, step)
        hot = jnp.where(iota((step, 256), 0) == ids - base, 1.0, 0.0).astype(BF16)
        return acc + dot(r.vocab_w[:, pl.ds(base, step)], hot)

    emb = lax.fori_loop(0, 16384 // step, look_up, jnp.zeros((64, 256), F32))
    r.emb_s[...] = emb.astype(BF16)
    x_emb = Exchange(gx, same(r.emb_s), slots(r.emb_r), r.emb_r, s.emb)
    x_emb.start()

    x_edges.arrive()
    x_state.arrive()
    to_smem.wait()

    def reorder(n, carry):
        zz = lax.div(n, 8)
        qq = lax.rem(n, 8)
        old = meta_m[batch_of(lax.div(qq, 2), zz, lax.rem(qq, 2)), 0, 5]
        r.edges_f[n] = r.edges_r[old].astype(F32)
        r.state_s[n] = r.state_r[old]
        return carry

    lax.fori_loop(0, 64, reorder, 0)
    x_zstate = Exchange(gz, lambda i: r.state_s.at[rows(i * 8, 8)], slots(r.state_z), r.state_z, s.zstate)
    x_zstate.start()

    x_emb.arrive()
    own = jnp.sum(r.emb_r[...].astype(F32), axis=0)
    r.blk[...] = own.astype(BF16)
    x_stream = Exchange(gq, same(r.blk), slots(r.stream_r), r.stream_r, s.stream)
    x_stream.start()
    block_stats(own, r.st)
    x_stats = Exchange(gb, same(r.st), slots(r.st_r), r.st_r, s.stats)
    x_stats.start()

    x_prm.arrive()
    prm = jnp.concatenate([r.prm_r[2 * k] + r.prm_r[2 * k + 1] for k in range(NY)], axis=1)

    def shifted(normed, k, first):
        now = normed.astype(F32).reshape(8, 4, 8, 512)
        edge = jnp.concatenate([r.edges_f[:, k * 4 + i, :] for i in range(NY)], axis=1)
        before = jnp.concatenate([edge.reshape(8, 1, 8, 512), now[:, :3]], axis=1)
        delta = (before - now).reshape(256, 512)
        now = now.reshape(256, 512)
        return lambda n: (now + delta * prm[first + n : first + n + 1]).astype(BF16)

    last = jnp.logical_and(
        iota((64, 256), 0)
        == device_of(lax.shift_right_logical(lane_t, 5), lane_t & 7),
        slot == length - 1,
    )
    last = jnp.where(last, 1.0, 0.0).astype(BF16)

    def layer(x, k):
        normed = (x.T * prm[k : k + 1] + prm[2 + k : 3 + k]).astype(BF16)
        r.norm_t[...] = normed.astype(F32).T
        mine = r.norm_t[rows(q * 64, 64), :].astype(BF16)
        r.new_edges_o[k] = dot(last, mine, 1).astype(BF16)
        return normed

    x_stream.arrive()
    x_stats.arrive()
    mean, var = join(r.st_r, 64.0, 4096.0)
    scaled = (r.stream_r[...].astype(F32).reshape(512, 256) - mean) * lax.rsqrt(var + EPS_LN)
    mixed = shifted(layer(scaled, 0), 0, 4)
    x_maps.arrive()
    x_low.arrive()
    for n in range(5):
        w = r.maps_w[n] if n < 4 else r.low_w[...]
        r.part_s[n] = dot(mixed(n), w.reshape(512, 128)).astype(BF16)
    x_part = Exchange(gz, lambda i: r.part_s.at[:, rows(i * 32, 32)], slots(r.part_r), r.part_r, s.part)
    x_part.start()

    x_zstate.arrive()
    left = iota((32, 128), 1) < 64
    for n in range(8):
        tile = r.state_z[:, n].astype(F32).reshape(64, 128)
        turn = pltpu.roll(tile, 64, 1)
        blocks = [
            jnp.where(left, tile[0:32], 0.0),
            jnp.where(left, turn[0:32], 0.0),
            jnp.where(left, 0.0, turn[32:64]),
            jnp.where(left, 0.0, tile[32:64]),
        ]
        r.bd[n] = jnp.concatenate(blocks, axis=0).astype(BF16)
    lens8 = r.table[rows(z * 8, 8), :][:, 4:5].astype(jnp.int32)

    x_part.arrive()
    proj = jnp.sum(r.part_r[...].astype(F32), axis=0)
    low = jnp.tanh(proj[4]).astype(BF16)
    decay = jnp.exp(-jnp.exp(r.floor[pl.ds(q, 1), :] + dot(low, r.second[:, lanes(q * 128, 128)])))
    rec = [proj[0, 8 * j : 8 * j + 8] for j in range(4)]
    key = [proj[1, 8 * j : 8 * j + 8] for j in range(4)]
    val = [proj[2, 8 * j : 8 * j + 8] for j in range(4)]
    dec = [decay[8 * j : 8 * j + 8] for j in range(4)]
    bonus = r.bonus[pl.ds(q, 1), :]
    alive = [lens8 > j for j in range(4)]
    seen, inner = [], []
    for j in range(4):
        acc = head_sum(rec[j] * bonus * key[j]) * val[j]
        run = rec[j]
        for i in range(j - 1, -1, -1):
            acc = acc + head_sum(run * key[i]) * val[i]
            run = run * dec[i]
        seen.append(run)
        inner.append(acc)
    row_q = iota((32, 128), 0) & 7

    def spread(x):
        return jnp.concatenate([jnp.where(row_q == n, x, 0.0) for n in range(8)], axis=1)

    wide = spread(jnp.concatenate(seen, axis=0))
    high, rest = split(wide)
    bd = r.bd[...].reshape(1024, 128)
    wkv = dot(high, bd) + dot(rest, bd) + jnp.concatenate(inner, axis=0)
    mu = head_sum(wkv) * (1.0 / 64)
    dev = wkv - mu
    spr = head_sum(dev * dev) * (1.0 / 64)
    grouped = dev * lax.rsqrt(spr + EPS_GN) * r.gn_gain[pl.ds(q, 1), :] + r.gn_bias[pl.ds(q, 1), :]
    gate = proj[3]
    r.gated_s[...] = (grouped * (gate * jax.nn.sigmoid(gate))).astype(BF16)
    x_gated = Exchange(gz, same(r.gated_s), slots(r.gated_r), r.gated_r, s.gated)
    x_gated.start()

    tail, keys = jnp.ones((8, 128), F32), []
    for j in range(3, -1, -1):
        keys.append(jnp.where(alive[j], key[j] * tail, 0.0))
        tail = jnp.where(alive[j], tail * dec[j], tail)
    keys = spread(jnp.concatenate(keys[::-1], axis=0)).T
    vals = jnp.concatenate(val, axis=0)
    kh, kl = split(keys)
    vh, vl = split(vals)
    outer = dot(kh, vh) + dot(kl, vh) + dot(kh, vl)
    tail = tail.T
    for n in range(8):
        new = outer[n * 128 : n * 128 + 128] + tail[:, n : n + 1] * r.bd[n].astype(F32)
        turn = pltpu.roll(new, 64, 1)
        top = jnp.where(left, new[0:32], turn[32:64])
        bottom = jnp.where(left, turn[64:96], new[96:128])
        r.new_s[n] = jnp.concatenate([top, bottom], axis=0).astype(BF16)
    x_new = Exchange(gq, lambda i: r.new_s.at[i], lambda m: r.states_o.at[m], r.states_o, s.new)
    x_new.start()

    x_emit.arrive()
    x_gated.arrive()
    att = dot(r.emit_w[...].reshape(512, 128), r.gated_r[...].reshape(256, 128), 1)
    r.att_s[...] = att.astype(BF16).reshape(8, 64, 256)
    x_att = Exchange(gq, lambda i: r.att_s.at[i], slots(r.att_r), r.att_r, s.att)
    x_att.start()
    x_att.arrive()
    r.attx_s[...] = jnp.sum(r.att_r[...].astype(F32), axis=0).astype(BF16)
    x_attx = Exchange(gx, same(r.attx_s), slots(r.attx_r), r.attx_r, s.attx)
    x_attx.start()
    x_attx.arrive()
    two = r.blk[...].astype(F32) + jnp.sum(r.attx_r[...].astype(F32), axis=0)
    r.two[...] = two
    r.dev_s[...] = block_stats(two, r.st2).astype(BF16)
    x_dev = Exchange(gq, same(r.dev_s), slots(r.dev_r), r.dev_r, s.dev2)
    x_dev.start()
    x_stats2 = Exchange(gb, same(r.st2), slots(r.st2_r), r.st2_r, s.stats2)
    x_stats2.start()
    x_dev.arrive()
    x_stats2.arrive()
    mean, var = join(r.st2_r, 64.0, 4096.0)
    scale = lax.rsqrt(var + EPS_LN)
    blocks = []
    for n in range(8):
        off = r.st2_r[batch_of(n // 2, z, n % 2)][0:1] - mean
        blocks.append((r.dev_r[n].astype(F32) + off) * scale)
    mixed = shifted(layer(jnp.concatenate(blocks, axis=0), 1), 1, 9)

    x_look.arrive()
    x_acc.arrive()
    up = dot(mixed(0), r.look_w[...].reshape(512, 512))
    r.up_s[...] = up.astype(BF16).reshape(8, 32, 512)
    x_up = Exchange(gz, lambda i: r.up_s.at[i], slots(r.up_r), r.up_r, s.up)
    x_up.start()
    rec = dot(mixed(1), r.acc_w[...].reshape(512, 128)).T
    r.rec_s[...] = rec.astype(BF16).reshape(8, 16, 256)
    x_rec = Exchange(gz, lambda i: r.rec_s.at[i], slots(r.rec_r), r.rec_r, s.rec)
    x_rec.start()
    x_up.arrive()
    up = jnp.maximum(jnp.sum(r.up_r[...].astype(F32), axis=0), 0.0)
    up = jnp.where(jnp.logical_and(c == 1, iota(up.shape, 1) < 128), 0.0, up * up)
    r.units_s[...] = up.astype(BF16)
    x_units = Exchange(gz, same(r.units_s), slots(r.units_r), r.units_r, s.units)
    x_units.start()
    x_rec.arrive()
    r.sig_s[...] = jax.nn.sigmoid(jnp.sum(r.rec_r[...].astype(F32), axis=0))

    def far_copy(k):
        return pltpu.make_async_remote_copy(
            src_ref=r.sig_s,
            dst_ref=r.sig_r.at[lax.rem(z, NX)],
            send_sem=s.sig.at[0],
            recv_sem=s.sig.at[1],
            device_id=dest(k),
            device_id_type=MESH,
        )

    for k in range(4):
        here = jnp.logical_and(dest_here, h == k)

        @pl.when(jnp.logical_not(here))
        def _():
            far_copy(k).start()

        @pl.when(here)
        def _():
            pltpu.make_async_copy(r.sig_s, r.sig_r.at[lax.rem(z, NX)], s.sig.at[1]).start()

    x_down.arrive()
    x_units.arrive()
    val = dot(r.down_w[...].reshape(512, 512), r.units_r[...].reshape(256, 512), 1)
    r.val_s[...] = val.astype(BF16).reshape(8, 64, 256)
    x_val = Exchange(gq, lambda i: r.val_s.at[i], slots(r.val_r), r.val_r, s.val)
    x_val.start()
    x_val.arrive()
    r.valx_s[...] = jnp.sum(r.val_r[...].astype(F32), axis=0).astype(BF16)
    x_valx = Exchange(gx, same(r.valx_s), slots(r.valx_r), r.valx_r, s.valx)
    x_valx.start()
    pltpu.make_async_copy(r.sig_r, r.sig_r, s.sig.at[1]).wait()
    x_valx.arrive()
    value = jnp.sum(r.valx_r[...].astype(F32), axis=0)
    result = r.two[...] + r.sig_r[...].reshape(64, 256) * value
    r.hidden_o[...] = jnp.where(slot < length, result, 0.0).T

    x_new.arrive()
    for k in range(4):

        @pl.when(jnp.logical_not(jnp.logical_and(dest_here, h == k)))
        def _():
            far_copy(k).wait_send()

    for x in (
        x_meta, x_prm, x_edges, x_state, x_low, x_maps, x_emit, x_look, x_acc, x_down, x_emb, x_zstate, x_stream,
        x_stats, x_part, x_gated, x_new, x_att, x_attx, x_dev, x_stats2, x_up, x_rec, x_units, x_val, x_valx,
    ):
        x.drain()


def local(
    query_symbol_numbers,
    alive_span_sizes,
    former_positions,
    previous_normed_vectors,
    memory_matrices,
    vocabulary_vectors,
    standardize_scales,
    standardize_shifts,
    timemix_blend_factors,
    timemix_linear_maps,
    forgetting_first_lowrank,
    forgetting_second_lowrank,
    forgetting_loglog_floor,
    current_reward_factor,
    perspan_standardize_scale,
    perspan_standardize_shift,
    timemix_emit_matrix,
    feedforward_blend_factors,
    feedforward_lookup_matrix,
    feedforward_accept_matrix,
    feedforward_emit_matrix,
):
    edges = (
        previous_normed_vectors.reshape(2, NY, NZ, 128).transpose(2, 0, 1, 3).reshape(NZ, 8, 128)
    )
    state = memory_matrices.reshape(16, 2, 32, 64).transpose(0, 2, 1, 3).reshape(64, 8, 128)
    spaces = {
        "S": pl.BlockSpec(memory_space=pltpu.SMEM),
        "V": VM,
        "A": ANY,
    }
    hidden, new_edges, states = pl.pallas_call(
        kernel,
        out_shape=[
            jax.ShapeDtypeStruct((256, 64), F32),
            jax.ShapeDtypeStruct((2, 64, 64), BF16),
            jax.ShapeDtypeStruct((8, 64, 128), BF16),
        ],
        in_specs=[spaces[k] for k in SPACES],
        out_specs=[VM] * 3,
        scratch_shapes=[pltpu.VMEM(shape, dtype) for _, shape, dtype in SCRATCH]
        + [DMA((2,)) for _ in SEMS]
        + [DMA((2,)), DMA(()), DMA(()), pltpu.SMEM((64, 1, 128), jnp.int32)],
        compiler_params=pltpu.CompilerParams(
            collective_id=0, has_side_effects=True, vmem_limit_bytes=48 << 20
        ),
        name="layer",
    )(
        query_symbol_numbers,
        alive_span_sizes,
        former_positions,
        standardize_scales,
        standardize_shifts,
        timemix_blend_factors,
        feedforward_blend_factors,
        edges,
        state,
        forgetting_first_lowrank,
        timemix_linear_maps,
        timemix_emit_matrix,
        feedforward_lookup_matrix,
        feedforward_accept_matrix,
        feedforward_emit_matrix,
        vocabulary_vectors,
        forgetting_second_lowrank,
        forgetting_loglog_floor.reshape(8, 128),
        current_reward_factor.reshape(8, 128),
        perspan_standardize_scale.reshape(8, 128),
        perspan_standardize_shift.reshape(8, 128),
    )
    hidden = hidden.reshape(NZ, 4, NY, NC, 64).transpose(2, 0, 3, 1, 4).reshape(64, 4, 64)
    states = states.reshape(16, 32, 2, 64).transpose(0, 2, 1, 3).reshape(1, 16, 64, 64)
    return hidden, new_edges, states


def solution(mesh):
    return jax.shard_map(
        local,
        mesh=mesh,
        in_specs=(
            P("batch", None),
            P("batch"),
            P("batch"),
            P(None, "batch", None),
            P("batch", "head", None, None),
            P("batch", "head"),
            P(None, "batch"),
            P(None, "batch"),
            P(None, "batch"),
            P(None, "batch", "head"),
            P("batch", None),
            P(None, "head"),
            P("head"),
            P("head"),
            P("head"),
            P("head"),
            P("batch", "head"),
            P(None, "batch"),
            P("batch", "head"),
            P("batch", None),
            P("batch", "head"),
        ),
        out_specs=(P(None, None, "batch"), P(None, None, "batch"), P("batch", "head", None, None)),
        check_vma=False,
    )
```

time: 1990 us -> 132 us (0.07)
  blocking collectives: 1170 us -> 0 us
  waiting for transfers between devices: 667 us -> 0 us
  Pallas kernels: 0 us -> 110 us
  local copies, waits for them, and re-layouts: 76.2 us -> 18.7 us
  matrix products: 30.9 us -> 0 us
    psum x7 -> x0, blocking collectives: 1020 us -> none  [the longest x2 492 us: normalize(): lax.psum(jnp.sum(centered * centered, axis=-1), 'batch') / EMBEDDING_DIM]
    unnamed x7 -> x0, waiting for transfers between devices: 380 us -> none
    all_gather x2 -> x0, waiting for transfers between devices: 164 us -> none  [the longest x1 96.7 us: local(): piece = lax.all_gather(memory_matrices, 'batch', axis=0, tiled=True)]
    reduce_scatter x1 -> x0, waiting for transfers between devices: 124 us -> none  [local(): lax.psum_scatter(lax.dot_general(part, mixed_two[1], (((0,), (1,)), ((),...]
    pallas_call x0 -> x1, Pallas kernels: none -> 110 us  [local(): pl.pallas_call(kernel, out_shape=[jax.ShapeDtypeStruct((256, 64), F32), j...]
    all_gather x2 -> x0, blocking collectives: 91.7 us -> none  [the longest x1 48.6 us: local(): lax.all_gather(gated, 'batch', axis=0, tiled=True)]
    unnamed x1 -> x0, blocking collectives: 55.7 us -> none
    dot_general x12 -> x0, matrix products: 30.9 us -> none  [the longest x1 15.5 us: local(): jnp.dot(select, piece.reshape(rows, state_width), preferred_element_type=...]
  transfers between devices with their start and end apart: 6 -> 0, of which waited for: 5 -> 0; matrix products, arithmetic and copies ran while one was open for 2% -> 0% of each run, Pallas kernels for 0% -> 0%
where the time goes in v2:
time: 132 us; the launch traced here: 131 us
  Pallas kernels  110 us (83%)
  local copies, waits for them, and re-layouts  18.7 us (14%)
  between operations  1.98 us (2%)
    pallas_call x1, Pallas kernels, local(): pl.pallas_call(kernel, out_shape=[jax.ShapeDtypeStruct((256, 64), F32), j...  110 us
    unnamed x36, local copies, waits for them, and re-layouts  15.7 us

profile of v2, /device:TPU:1, one launch (start us, length us, event | category | flops | bytes accessed | tf_op | source)
XLA Modules:
  0.0 131.0 jit_solution(1204052130926330358)
XLA Ops:
  1.9 0.7 copy.32
  2.7 1.2 copy.31
  3.9 0.1 reshape.45.refs_8_
  4.0 1.6 %copy-done = bf16[64,16384]{1,0:T(8,128)(2,1)S(1)} copy-done((bf16[64,16384]{1,0:T(8,128)(2,1)S(1)}, bf16[64,16384]{1,0:T(8,128)(2,1)}, u32[]{:S(2)}) %copy-start) | copy-done | bytes 2097176
  5.6 1.0 copy-done.1
  6.6 1.0 copy-done.2
  7.7 1.0 copy-done.3
  8.7 1.0 copy-done.4
  9.7 0.9 copy-done.5
  10.7 0.9 copy-done.6
  11.6 0.7 copy-done.7
  12.3 0.7 copy-done.8
  13.0 0.7 copy-done.9
  13.7 0.7 copy-done.10
  14.4 0.7 copy-done.11
  15.1 0.7 copy-done.12
  15.7 0.7 copy-done.13
  16.4 0.7 copy-done.14
  17.1 0.7 copy-done.15
  17.8 0.7 copy-done.16
  18.4 110.4 %layer.1 = (f32[256,64]{1,0:T(8,128)S(1)}, bf16[2,64,64]{2,1,0:T(8,128)(2,1)S(1)}, bf16[8,64,128]{2,1,0:T(8,128)(2,1)S(1)}) custom-call(s32[1,4]{1,0:T(1,128)S(1)} %copy-done.16, s32[1]{0:T(128)S(6)} %copy.34.refs_1_, s32[1]{0:T(128)S(6)} %copy.35.refs_2_, f32[2,64]{1,0:T(2,128)S(1)} %copy-done.13, f32[2,64]{1,0:T(2,128)S(1)} %copy-done.14, ...), custom_call_target="tpu_custom_call" | custom-call | tf_op jit(solution)/shard_map/layer/pallas_call | solution.py:617
  128.8 0.7 copy.26
  129.7 0.8 copy.27
  130.4 0.6 copy.36
  (19 shorter events, 0.2 us)
Async XLA Ops:
  4.0 1.6 %copy-start = (bf16[64,16384]{1,0:T(8,128)(2,1)S(1)}, bf16[64,16384]{1,0:T(8,128)(2,1)}, u32[]{:S(2)}) copy-start(bf16[64,16384]{1,0:T(8,128)(2,1)} %refs_15_.1) | copy-start | bytes 6291460
  5.6 1.0 copy-start.1
  6.6 1.0 copy-start.2
  7.7 1.0 copy-start.3
  8.7 1.0 copy-start.4
  9.7 0.9 copy-start.5
  10.7 0.9 copy-start.6
  11.6 0.7 copy-start.7
  12.3 0.7 copy-start.8
  13.0 0.7 copy-start.9
  13.7 0.7 copy-start.10
  14.4 0.7 copy-start.11
  15.0 0.7 copy-start.12
  15.7 0.7 copy-start.13
  16.4 0.7 copy-start.14
  17.1 0.7 copy-start.15
  17.8 0.7 copy-start.16

commit v3 on v2

--- a/solution.py
+++ b/solution.py
@@ -95,11 +95,8 @@
         pltpu.make_async_copy(self.whole, self.whole, self.sems.at[1]).wait()
 
     def drain(self):
-        part = self.dst(0)
-        for _ in range(1):
-            self.g.each(
-                lambda p, i: pltpu.make_async_copy(part, part, self.sems.at[0]).wait()
-            )
+        part = self.dst(pl.ds(0, self.g.n - 1))
+        pltpu.make_async_copy(part, part, self.sems.at[0]).wait()
 
 
 def lanes(i, n):
@@ -155,14 +152,37 @@
     "ids", "lens", "pos", "gains", "biases", "mixes", "mixes2", "edges", "state", "low", "maps",
     "emit", "look", "acc", "down", "vocab", "second", "floor", "bonus", "gn_gain", "gn_bias",
 ]
-SPACES = ["S"] * 3 + ["V"] * 6 + ["A"] * 7 + ["V"] * 5
+LOCAL = [
+    "ids", "lens", "pos", "gains", "biases", "mixes", "mixes2", "edges", "state", "second",
+    "floor", "bonus", "gn_gain", "gn_bias",
+]
+LOCAL_SHAPES = [
+    ((1, 4), jnp.int32),
+    ((1,), jnp.int32),
+    ((1,), jnp.int32),
+    ((2, 64), F32),
+    ((2, 64), F32),
+    ((5, 64), F32),
+    ((2, 64), F32),
+    ((2, 4096), BF16),
+    ((16, 64, 64), BF16),
+    ((128, 128), BF16),
+    ((8, 128), F32),
+    ((8, 128), F32),
+    ((8, 128), F32),
+    ((8, 128), F32),
+]
 OUTPUTS = ["hidden", "new_edges", "states"]
 SCRATCH = [
     ("meta_s", (1, 128), jnp.int32),
     ("meta_r", (64, 1, 128), jnp.int32),
     ("prm_s", (16, 128), F32),
     ("prm_r", (8, 16, 128), F32),
+    ("edges_s", (8, 8, 128), BF16),
     ("edges_r", (64, 8, 128), BF16),
+    ("state_p", (64, 8, 128), BF16),
+    ("state_n", (8, 64, 128), BF16),
+    ("out", (256, 64), F32),
     ("edges_f", (64, 8, 128), F32),
     ("state_r", (64, 8, 128), BF16),
     ("state_s", (64, 8, 128), BF16),
@@ -224,11 +244,12 @@
 def kernel(*refs):
     r, s = Refs(), Refs()
     names = INPUTS + OUTPUTS + [n for n, _, _ in SCRATCH]
+    refs, meta_m = refs[:-1], refs[-1]
+    refs, fetched = refs[: -len(LOCAL)], refs[-len(LOCAL) :]
     for name, ref in zip(names, refs):
         setattr(r, name + ("_o" if name in OUTPUTS else ""), ref)
-    for name, ref in zip(SEMS + ["sig", "vocab", "smem"], refs[len(names) :]):
+    for name, ref in zip(SEMS + ["sig", "vocab", "smem", "local"], refs[len(names) :]):
         setattr(s, name, ref)
-    meta_m = refs[-1]
     h, b, y, z, c, q = place()
     gb, gq, gx, gz = Group("b"), Group("q"), Group("x"), Group("z")
 
@@ -248,8 +269,18 @@
         def _():
             pl.semaphore_signal(sem, inc=1, device_id=far, device_id_type=MESH)
 
+    fetch = {}
+    for n, (name, ref) in enumerate(zip(LOCAL, fetched)):
+        whole = getattr(r, name)
+        if name == "second":
+            whole = whole.at[:, lanes(q * 128, 128)]
+        fetch[name] = pltpu.make_async_copy(whole, ref, s.local.at[n])
+        fetch[name].start()
+        setattr(r, name, ref)
     vocab_in = pltpu.make_async_copy(r.vocab, r.vocab_w, s.vocab)
     vocab_in.start()
+    for name in LOCAL[:7]:
+        fetch[name].wait()
     lane = iota((1, 128), 1)
     meta = jnp.where(lane == 4, r.lens[0], jnp.where(lane == 5, r.pos[0], 0))
     for j in range(4):
@@ -263,6 +294,18 @@
     prm = r.prm_s[...]
     r.prm_s[...] = jnp.where(c == 0, prm, pltpu.roll(prm, 64, 1))
 
+    fetch["edges"].wait()
+    old = r.edges[...].astype(F32)
+    for k in range(NZ):
+        tiles = [old[:, (i * NZ + k) * 128 : (i * NZ + k) * 128 + 128] for i in range(NY)]
+        r.edges_s[k] = jnp.concatenate(tiles, axis=0).astype(BF16)
+    fetch["state"].wait()
+    for k in range(16):
+        tile = r.state[k].astype(F32)
+        tile = jnp.concatenate([tile[0:32], tile[32:64]], axis=1).astype(BF16)
+        for i in range(4):
+            r.state_p[k * 4 + i] = tile[i * 8 : i * 8 + 8]
+
     pl.semaphore_wait(sem, gb.n - 1 + gx.n - 1 + 3 * (1 - dest_here.astype(jnp.int32)))
 
     def same(ref):
@@ -274,11 +317,11 @@
     x_meta = Exchange(gb, same(r.meta_s), slots(r.meta_r), r.meta_r, s.meta)
     x_prm = Exchange(gq, same(r.prm_s), slots(r.prm_r), r.prm_r, s.prm)
     x_edges = Exchange(
-        gb, lambda i: r.edges.at[lax.rem(lax.div(i, NC), NZ)], slots(r.edges_r), r.edges_r, s.edges
+        gb, lambda i: r.edges_s.at[lax.rem(lax.div(i, NC), NZ)], slots(r.edges_r), r.edges_r, s.edges
     )
     x_state = Exchange(
         gb,
-        lambda i: r.state.at[
+        lambda i: r.state_p.at[
             (lax.div(i, NC * NZ) * NC + lax.rem(i, NC)) * NZ + lax.rem(lax.div(i, NC), NZ)
         ],
         slots(r.state_r),
@@ -307,7 +350,7 @@
     x_down = Exchange(
         gq, lambda i: r.down.at[:, lanes(chunk_start(i), 512)], slots(r.down_w), r.down_w, s.down
     )
-    for x in (x_meta, x_prm, x_edges, x_state, x_maps, x_low, x_emit, x_look, x_acc, x_down):
+    for x in (x_meta, x_maps, x_low, x_prm, x_edges):
         x.start()
 
     x_meta.arrive()
@@ -339,7 +382,7 @@
     length = tok_rows[4:5].astype(jnp.int32)
 
     vocab_in.wait()
-    step = 1024
+    step = 4096
 
     def look_up(k, acc):
         base = pl.multiple_of(k * step, step)
@@ -350,22 +393,7 @@
     r.emb_s[...] = emb.astype(BF16)
     x_emb = Exchange(gx, same(r.emb_s), slots(r.emb_r), r.emb_r, s.emb)
     x_emb.start()
-
-    x_edges.arrive()
-    x_state.arrive()
-    to_smem.wait()
-
-    def reorder(n, carry):
-        zz = lax.div(n, 8)
-        qq = lax.rem(n, 8)
-        old = meta_m[batch_of(lax.div(qq, 2), zz, lax.rem(qq, 2)), 0, 5]
-        r.edges_f[n] = r.edges_r[old].astype(F32)
-        r.state_s[n] = r.state_r[old]
-        return carry
-
-    lax.fori_loop(0, 64, reorder, 0)
-    x_zstate = Exchange(gz, lambda i: r.state_s.at[rows(i * 8, 8)], slots(r.state_z), r.state_z, s.zstate)
-    x_zstate.start()
+    x_state.start()
 
     x_emb.arrive()
     own = jnp.sum(r.emb_r[...].astype(F32), axis=0)
@@ -376,12 +404,28 @@
     x_stats = Exchange(gb, same(r.st), slots(r.st_r), r.st_r, s.stats)
     x_stats.start()
 
+    x_edges.arrive()
+    x_state.arrive()
+    to_smem.wait()
+
+    def reorder(n, carry):
+        zz = lax.div(n, 8)
+        qq = lax.rem(n, 8)
+        old = meta_m[batch_of(lax.div(qq, 2), zz, lax.rem(qq, 2)), 0, 5]
+        r.edges_f[n] = r.edges_r[old].astype(F32)
+        r.state_s[n] = r.state_r[old]
+        return carry
+
+    lax.fori_loop(0, 64, reorder, 0)
+    x_zstate = Exchange(gz, lambda i: r.state_s.at[rows(i * 8, 8)], slots(r.state_z), r.state_z, s.zstate)
+    x_zstate.start()
+
     x_prm.arrive()
     prm = jnp.concatenate([r.prm_r[2 * k] + r.prm_r[2 * k + 1] for k in range(NY)], axis=1)
 
     def shifted(normed, k, first):
         now = normed.astype(F32).reshape(8, 4, 8, 512)
-        edge = jnp.concatenate([r.edges_f[:, k * 4 + i, :] for i in range(NY)], axis=1)
+        edge = jnp.concatenate([r.edges_f[:, i * 2 + k, :] for i in range(NY)], axis=1)
         before = jnp.concatenate([edge.reshape(8, 1, 8, 512), now[:, :3]], axis=1)
         delta = (before - now).reshape(256, 512)
         now = now.reshape(256, 512)
@@ -413,6 +457,8 @@
         r.part_s[n] = dot(mixed(n), w.reshape(512, 128)).astype(BF16)
     x_part = Exchange(gz, lambda i: r.part_s.at[:, rows(i * 32, 32)], slots(r.part_r), r.part_r, s.part)
     x_part.start()
+    for x in (x_emit, x_look, x_acc, x_down):
+        x.start()
 
     x_zstate.arrive()
     left = iota((32, 128), 1) < 64
@@ -430,8 +476,10 @@
 
     x_part.arrive()
     proj = jnp.sum(r.part_r[...].astype(F32), axis=0)
+    for name in LOCAL[9:]:
+        fetch[name].wait()
     low = jnp.tanh(proj[4]).astype(BF16)
-    decay = jnp.exp(-jnp.exp(r.floor[pl.ds(q, 1), :] + dot(low, r.second[:, lanes(q * 128, 128)])))
+    decay = jnp.exp(-jnp.exp(r.floor[pl.ds(q, 1), :] + dot(low, r.second[...])))
     rec = [proj[0, 8 * j : 8 * j + 8] for j in range(4)]
     key = [proj[1, 8 * j : 8 * j + 8] for j in range(4)]
     val = [proj[2, 8 * j : 8 * j + 8] for j in range(4)]
@@ -481,7 +529,7 @@
         top = jnp.where(left, new[0:32], turn[32:64])
         bottom = jnp.where(left, turn[64:96], new[96:128])
         r.new_s[n] = jnp.concatenate([top, bottom], axis=0).astype(BF16)
-    x_new = Exchange(gq, lambda i: r.new_s.at[i], lambda m: r.states_o.at[m], r.states_o, s.new)
+    x_new = Exchange(gq, lambda i: r.new_s.at[i], lambda m: r.state_n.at[m], r.state_n, s.new)
     x_new.start()
 
     x_emit.arrive()
@@ -558,6 +606,11 @@
     r.val_s[...] = val.astype(BF16).reshape(8, 64, 256)
     x_val = Exchange(gq, lambda i: r.val_s.at[i], slots(r.val_r), r.val_r, s.val)
     x_val.start()
+    x_new.arrive()
+    for k in range(16):
+        tile = r.state_n[k // 2].astype(F32)[(k % 2) * 32 : (k % 2) * 32 + 32]
+        r.states_o[k, 0:32] = tile[:, 0:64].astype(BF16)
+        r.states_o[k, 32:64] = tile[:, 64:128].astype(BF16)
     x_val.arrive()
     r.valx_s[...] = jnp.sum(r.val_r[...].astype(F32), axis=0).astype(BF16)
     x_valx = Exchange(gx, same(r.valx_s), slots(r.valx_r), r.valx_r, s.valx)
@@ -566,9 +619,11 @@
     x_valx.arrive()
     value = jnp.sum(r.valx_r[...].astype(F32), axis=0)
     result = r.two[...] + r.sig_r[...].reshape(64, 256) * value
-    r.hidden_o[...] = jnp.where(slot < length, result, 0.0).T
-
-    x_new.arrive()
+    r.out[...] = jnp.where(slot < length, result, 0.0).T
+    for k in range(64):
+        first = (k // 2 % NZ) * 32 + (k // 16) * 2 + k % 2
+        r.hidden_o[k] = r.out[pl.ds(first, 4, stride=8), :]
+
     for k in range(4):
 
         @pl.when(jnp.logical_not(jnp.logical_and(dest_here, h == k)))
@@ -605,29 +660,25 @@
     feedforward_accept_matrix,
     feedforward_emit_matrix,
 ):
-    edges = (
-        previous_normed_vectors.reshape(2, NY, NZ, 128).transpose(2, 0, 1, 3).reshape(NZ, 8, 128)
-    )
-    state = memory_matrices.reshape(16, 2, 32, 64).transpose(0, 2, 1, 3).reshape(64, 8, 128)
-    spaces = {
-        "S": pl.BlockSpec(memory_space=pltpu.SMEM),
-        "V": VM,
-        "A": ANY,
-    }
     hidden, new_edges, states = pl.pallas_call(
         kernel,
         out_shape=[
-            jax.ShapeDtypeStruct((256, 64), F32),
+            jax.ShapeDtypeStruct((64, 4, 64), F32),
             jax.ShapeDtypeStruct((2, 64, 64), BF16),
-            jax.ShapeDtypeStruct((8, 64, 128), BF16),
+            jax.ShapeDtypeStruct((16, 64, 64), BF16),
         ],
-        in_specs=[spaces[k] for k in SPACES],
+        in_specs=[ANY] * len(INPUTS),
         out_specs=[VM] * 3,
         scratch_shapes=[pltpu.VMEM(shape, dtype) for _, shape, dtype in SCRATCH]
         + [DMA((2,)) for _ in SEMS]
-        + [DMA((2,)), DMA(()), DMA(()), pltpu.SMEM((64, 1, 128), jnp.int32)],
+        + [DMA((2,)), DMA(()), DMA(()), DMA((len(LOCAL),))]
+        + [
+            (pltpu.SMEM if n < 3 else pltpu.VMEM)(shape, dtype)
+            for n, (shape, dtype) in enumerate(LOCAL_SHAPES)
+        ]
+        + [pltpu.SMEM((64, 1, 128), jnp.int32)],
         compiler_params=pltpu.CompilerParams(
-            collective_id=0, has_side_effects=True, vmem_limit_bytes=48 << 20
+            collective_id=0, has_side_effects=True, vmem_limit_bytes=67043328
         ),
         name="layer",
     )(
@@ -638,8 +689,8 @@
         standardize_shifts,
         timemix_blend_factors,
         feedforward_blend_factors,
-        edges,
-        state,
+        previous_normed_vectors.reshape(2, 4096),
+        memory_matrices.reshape(16, 64, 64),
         forgetting_first_lowrank,
         timemix_linear_maps,
         timemix_emit_matrix,
@@ -653,9 +704,7 @@
         perspan_standardize_scale.reshape(8, 128),
         perspan_standardize_shift.reshape(8, 128),
     )
-    hidden = hidden.reshape(NZ, 4, NY, NC, 64).transpose(2, 0, 3, 1, 4).reshape(64, 4, 64)
-    states = states.reshape(16, 32, 2, 64).transpose(0, 2, 1, 3).reshape(1, 16, 64, 64)
-    return hidden, new_edges, states
+    return hidden, new_edges, states.reshape(1, 16, 64, 64)
 
 
 def solution(mesh):

time: 132 us -> 102 us (0.77)
  Pallas kernels: 110 us -> 95.4 us
  local copies, waits for them, and re-layouts: 18.7 us -> 4.61 us
    pallas_call x1, Pallas kernels: 110 us -> 95.4 us  [local(): pl.pallas_call(kernel, out_shape=[jax.ShapeDtypeStruct((64, 4, 64), F32),...]
    unnamed x36 -> x3, local copies, waits for them, and re-layouts: 15.7 us -> 4.61 us
    reshape x4 -> x0, local copies, waits for them, and re-layouts: 1.48 us -> none  [the longest x2 1.34 us: local(): memory_matrices.reshape(16, 2, 32, 64).transpose(0, 2, 1, 3)]
    transpose x2 -> x0, local copies, waits for them, and re-layouts: 1.45 us -> none  [the longest x1 0.76 us: local(): states.reshape(16, 32, 2, 64).transpose(0, 2, 1, 3).reshape(1, 16, 64, 64)]
where the time goes in v3:
time: 102 us
  Pallas kernels  95.4 us (94%)
  local copies, waits for them, and re-layouts  4.61 us (5%)
  between operations  1.94 us (2%)
    pallas_call x1, Pallas kernels, local(): pl.pallas_call(kernel, out_shape=[jax.ShapeDtypeStruct((64, 4, 64), F32),...  95.4 us
    unnamed x3, local copies, waits for them, and re-layouts  4.61 us

profile of v3, /device:TPU:1, one launch (start us, length us, event | category | flops | bytes accessed | tf_op | source)
XLA Modules:
  0.0 102.0 jit_solution(10750435276514464532)
XLA Ops:
  1.9 95.4 %layer.1 = (f32[64,4,64]{2,1,0:T(4,128)}, bf16[2,64,64]{2,1,0:T(8,128)(2,1)}, bf16[16,64,64]{2,1,0:T(8,128)(2,1)}) custom-call(s32[1,4]{1,0:T(1,128)} %refs_0_.1, s32[1]{0:T(128)S(6)} %copy.27.refs_1_, s32[1]{0:T(128)S(6)} %copy.28.refs_2_, f32[2,64]{1,0:T(2,128)} %refs_3_.1, f32[2,64]{1,0:T(2,128)} %refs_4_.1, f32[5,64]{1,0:T(8,128)} %refs_5_.1, ...), custom_call_target="tpu_custom_call" | custom-call | tf_op jit(solution)/shard_map/layer/pallas_call | solution.py:663
  97.4 1.6 %copy.29 = f32[64,4,64]{2,1,0:T(4,128)} copy(f32[64,4,64]{2,1,0:T(4,128)} %get-tuple-element.12) | data formatting | bytes 131072
  99.0 1.4 %copy.30 = bf16[2,64,64]{2,1,0:T(8,128)(2,1)} copy(bf16[2,64,64]{2,1,0:T(8,128)(2,1)} %get-tuple-element.13) | data formatting | bytes 32768
  100.3 1.7 %copy.31 = bf16[1,16,64,64]{3,2,1,0:T(8,128)(2,1)} copy(bf16[1,16,64,64]{3,2,1,0:T(8,128)(2,1)} %bitcast.8) | data formatting | bytes 262144

commit v4 on v3

--- a/solution.py
+++ b/solution.py
@@ -201,40 +201,40 @@
     ("st", (2, 256), F32),
     ("st_r", (64, 2, 256), F32),
     ("stream_r", (8, 64, 256), BF16),
-    ("part_s", (5, 256, 128), BF16),
-    ("part_r", (8, 5, 32, 128), BF16),
+    ("part_s", (2, 5, 128, 128), BF16),
+    ("part_r", (2, 8, 5, 16, 128), BF16),
     ("bd", (8, 128, 128), BF16),
-    ("gated_s", (32, 128), BF16),
-    ("gated_r", (8, 32, 128), BF16),
+    ("gated_s", (2, 16, 128), BF16),
+    ("gated_r", (2, 8, 16, 128), BF16),
     ("new_s", (8, 64, 128), BF16),
-    ("att_s", (8, 64, 256), BF16),
-    ("att_r", (8, 64, 256), BF16),
-    ("attx_s", (64, 256), BF16),
-    ("attx_r", (NX, 64, 256), BF16),
+    ("att_s", (2, 8, 64, 128), BF16),
+    ("att_r", (2, 8, 64, 128), BF16),
+    ("attx_s", (2, 64, 128), BF16),
+    ("attx_r", (2, NX, 64, 128), BF16),
     ("two", (64, 256), F32),
     ("dev_s", (64, 256), BF16),
     ("st2", (2, 256), F32),
     ("st2_r", (64, 2, 256), F32),
     ("dev_r", (8, 64, 256), BF16),
-    ("up_s", (8, 32, 512), BF16),
-    ("up_r", (8, 32, 512), BF16),
+    ("up_s", (2, 8, 16, 512), BF16),
+    ("up_r", (2, 8, 16, 512), BF16),
     ("rec_s", (8, 16, 256), BF16),
     ("rec_r", (8, 16, 256), BF16),
-    ("units_s", (32, 512), BF16),
-    ("units_r", (8, 32, 512), BF16),
+    ("units_s", (2, 16, 512), BF16),
+    ("units_r", (2, 8, 16, 512), BF16),
     ("sig_s", (16, 256), F32),
     ("sig_r", (4, 16, 256), F32),
-    ("val_s", (8, 64, 256), BF16),
-    ("val_r", (8, 64, 256), BF16),
-    ("valx_s", (64, 256), BF16),
-    ("valx_r", (NX, 64, 256), BF16),
+    ("val_s", (2, 8, 64, 128), BF16),
+    ("val_r", (2, 8, 64, 128), BF16),
+    ("valx_s", (2, 64, 128), BF16),
+    ("valx_r", (2, NX, 64, 128), BF16),
     ("norm_t", (512, 256), F32),
 ]
 SEMS = [
     "meta", "prm", "edges", "state", "zstate", "low", "maps", "emit", "look", "acc", "down", "emb",
-    "stats", "stream", "part", "gated", "new", "att", "attx", "stats2", "dev2", "up", "rec",
-    "units", "val", "valx",
+    "stats", "stream", "new", "stats2", "dev2", "rec",
 ]
+HALVES = ["part", "gated", "att", "attx", "up", "units", "val", "valx"]
 
 
 class Refs:
@@ -248,7 +248,7 @@
     refs, fetched = refs[: -len(LOCAL)], refs[-len(LOCAL) :]
     for name, ref in zip(names, refs):
         setattr(r, name + ("_o" if name in OUTPUTS else ""), ref)
-    for name, ref in zip(SEMS + ["sig", "vocab", "smem", "local"], refs[len(names) :]):
+    for name, ref in zip(SEMS + HALVES + ["sig", "vocab", "smem", "local"], refs[len(names) :]):
         setattr(s, name, ref)
     h, b, y, z, c, q = place()
     gb, gq, gx, gz = Group("b"), Group("q"), Group("x"), Group("z")
@@ -365,7 +365,7 @@
         return (lax.shift_right_logical(qq, 1) * NZ + zz) * NC + (qq & 1)
 
     tok = iota((256, 64), 0)
-    by_tok = device_of(lax.shift_right_logical(tok, 5), tok & 7) == iota((256, 64), 1)
+    by_tok = device_of(lax.shift_right_logical(tok, 4) & 7, tok & 7) == iota((256, 64), 1)
     by_tok = jnp.where(by_tok, 1.0, 0.0).astype(BF16)
     cols = dot(by_tok, high) * 256.0 + dot(by_tok, lowb)
     req = iota((64, 64), 0)
@@ -374,7 +374,7 @@
     r.table[...] = dot(by_req, lowb)
     tok_rows = cols.T
     lane_t = iota((1, 256), 1)
-    slot = lax.shift_right_logical(lane_t, 3) & 3
+    slot = lax.shift_right_logical(lane_t, 7) * 2 + (lax.shift_right_logical(lane_t, 3) & 1)
     ids = tok_rows[0:1]
     for j in range(1, 4):
         ids = jnp.where(slot == j, tok_rows[j : j + 1], ids)
@@ -424,16 +424,32 @@
     prm = jnp.concatenate([r.prm_r[2 * k] + r.prm_r[2 * k + 1] for k in range(NY)], axis=1)
 
     def shifted(normed, k, first):
-        now = normed.astype(F32).reshape(8, 4, 8, 512)
+        now = normed.astype(F32).reshape(2, 8, 2, 8, 512)
         edge = jnp.concatenate([r.edges_f[:, i * 2 + k, :] for i in range(NY)], axis=1)
-        before = jnp.concatenate([edge.reshape(8, 1, 8, 512), now[:, :3]], axis=1)
-        delta = (before - now).reshape(256, 512)
-        now = now.reshape(256, 512)
-        return lambda n: (now + delta * prm[first + n : first + n + 1]).astype(BF16)
+        before = [
+            jnp.concatenate([edge.reshape(8, 1, 8, 512), now[0, :, :1]], axis=1).reshape(128, 512),
+            jnp.concatenate([now[0, :, 1:], now[1, :, :1]], axis=1).reshape(128, 512),
+        ]
+        now = [now[k].reshape(128, 512) for k in range(2)]
+        delta = [before[k] - now[k] for k in range(2)]
+        return lambda n, k: (now[k] + delta[k] * prm[first + n : first + n + 1]).astype(BF16)
+
+    def halves(group, name, src):
+        got, sems = getattr(r, name + "_r"), getattr(s, name)
+        return [
+            Exchange(
+                group,
+                lambda i, k=k: src(k, i),
+                lambda m, k=k: got.at[k, m],
+                got.at[k],
+                sems.at[k],
+            )
+            for k in range(2)
+        ]
 
     last = jnp.logical_and(
         iota((64, 256), 0)
-        == device_of(lax.shift_right_logical(lane_t, 5), lane_t & 7),
+        == device_of(lax.shift_right_logical(lane_t, 4) & 7, lane_t & 7),
         slot == length - 1,
     )
     last = jnp.where(last, 1.0, 0.0).astype(BF16)
@@ -452,11 +468,12 @@
     mixed = shifted(layer(scaled, 0), 0, 4)
     x_maps.arrive()
     x_low.arrive()
-    for n in range(5):
-        w = r.maps_w[n] if n < 4 else r.low_w[...]
-        r.part_s[n] = dot(mixed(n), w.reshape(512, 128)).astype(BF16)
-    x_part = Exchange(gz, lambda i: r.part_s.at[:, rows(i * 32, 32)], slots(r.part_r), r.part_r, s.part)
-    x_part.start()
+    x_part = halves(gz, "part", lambda k, i: r.part_s.at[k, :, rows(i * 16, 16)])
+    for k in range(2):
+        for n in range(5):
+            w = r.maps_w[n] if n < 4 else r.low_w[...]
+            r.part_s[k, n] = dot(mixed(n, k), w.reshape(512, 128)).astype(BF16)
+        x_part[k].start()
     for x in (x_emit, x_look, x_acc, x_down):
         x.start()
 
@@ -474,44 +491,48 @@
         r.bd[n] = jnp.concatenate(blocks, axis=0).astype(BF16)
     lens8 = r.table[rows(z * 8, 8), :][:, 4:5].astype(jnp.int32)
 
-    x_part.arrive()
-    proj = jnp.sum(r.part_r[...].astype(F32), axis=0)
     for name in LOCAL[9:]:
         fetch[name].wait()
-    low = jnp.tanh(proj[4]).astype(BF16)
-    decay = jnp.exp(-jnp.exp(r.floor[pl.ds(q, 1), :] + dot(low, r.second[...])))
-    rec = [proj[0, 8 * j : 8 * j + 8] for j in range(4)]
-    key = [proj[1, 8 * j : 8 * j + 8] for j in range(4)]
-    val = [proj[2, 8 * j : 8 * j + 8] for j in range(4)]
-    dec = [decay[8 * j : 8 * j + 8] for j in range(4)]
-    bonus = r.bonus[pl.ds(q, 1), :]
+    floor, bonus, gn_gain, gn_bias = (
+        ref[pl.ds(q, 1), :] for ref in (r.floor, r.bonus, r.gn_gain, r.gn_bias)
+    )
     alive = [lens8 > j for j in range(4)]
-    seen, inner = [], []
-    for j in range(4):
-        acc = head_sum(rec[j] * bonus * key[j]) * val[j]
-        run = rec[j]
-        for i in range(j - 1, -1, -1):
-            acc = acc + head_sum(run * key[i]) * val[i]
-            run = run * dec[i]
-        seen.append(run)
-        inner.append(acc)
-    row_q = iota((32, 128), 0) & 7
 
     def spread(x):
+        row_q = iota(x.shape, 0) & 7
         return jnp.concatenate([jnp.where(row_q == n, x, 0.0) for n in range(8)], axis=1)
 
-    wide = spread(jnp.concatenate(seen, axis=0))
-    high, rest = split(wide)
     bd = r.bd[...].reshape(1024, 128)
-    wkv = dot(high, bd) + dot(rest, bd) + jnp.concatenate(inner, axis=0)
-    mu = head_sum(wkv) * (1.0 / 64)
-    dev = wkv - mu
-    spr = head_sum(dev * dev) * (1.0 / 64)
-    grouped = dev * lax.rsqrt(spr + EPS_GN) * r.gn_gain[pl.ds(q, 1), :] + r.gn_bias[pl.ds(q, 1), :]
-    gate = proj[3]
-    r.gated_s[...] = (grouped * (gate * jax.nn.sigmoid(gate))).astype(BF16)
-    x_gated = Exchange(gz, same(r.gated_s), slots(r.gated_r), r.gated_r, s.gated)
-    x_gated.start()
+    rec, key, val, dec = [], [], [], []
+    x_gated = halves(gz, "gated", lambda k, i: r.gated_s.at[k])
+    for k in range(2):
+        x_part[k].arrive()
+        proj = jnp.sum(r.part_r[k].astype(F32), axis=0)
+        low = jnp.tanh(proj[4]).astype(BF16)
+        decay = jnp.exp(-jnp.exp(floor + dot(low, r.second[...])))
+        for j in range(2):
+            rec.append(proj[0, 8 * j : 8 * j + 8])
+            key.append(proj[1, 8 * j : 8 * j + 8])
+            val.append(proj[2, 8 * j : 8 * j + 8])
+            dec.append(decay[8 * j : 8 * j + 8])
+        seen, inner = [], []
+        for j in range(2 * k, 2 * k + 2):
+            acc = head_sum(rec[j] * bonus * key[j]) * val[j]
+            run = rec[j]
+            for i in range(j - 1, -1, -1):
+                acc = acc + head_sum(run * key[i]) * val[i]
+                run = run * dec[i]
+            seen.append(run)
+            inner.append(acc)
+        high, rest = split(spread(jnp.concatenate(seen, axis=0)))
+        wkv = dot(high, bd) + dot(rest, bd) + jnp.concatenate(inner, axis=0)
+        mu = head_sum(wkv) * (1.0 / 64)
+        dev = wkv - mu
+        spr = head_sum(dev * dev) * (1.0 / 64)
+        grouped = dev * lax.rsqrt(spr + EPS_GN) * gn_gain + gn_bias
+        gate = proj[3]
+        r.gated_s[k] = (grouped * (gate * jax.nn.sigmoid(gate))).astype(BF16)
+        x_gated[k].start()
 
     tail, keys = jnp.ones((8, 128), F32), []
     for j in range(3, -1, -1):
@@ -533,17 +554,22 @@
     x_new.start()
 
     x_emit.arrive()
-    x_gated.arrive()
-    att = dot(r.emit_w[...].reshape(512, 128), r.gated_r[...].reshape(256, 128), 1)
-    r.att_s[...] = att.astype(BF16).reshape(8, 64, 256)
-    x_att = Exchange(gq, lambda i: r.att_s.at[i], slots(r.att_r), r.att_r, s.att)
-    x_att.start()
-    x_att.arrive()
-    r.attx_s[...] = jnp.sum(r.att_r[...].astype(F32), axis=0).astype(BF16)
-    x_attx = Exchange(gx, same(r.attx_s), slots(r.attx_r), r.attx_r, s.attx)
-    x_attx.start()
-    x_attx.arrive()
-    two = r.blk[...].astype(F32) + jnp.sum(r.attx_r[...].astype(F32), axis=0)
+    x_att = halves(gq, "att", lambda k, i: r.att_s.at[k, i])
+    x_attx = halves(gx, "attx", lambda k, i: r.attx_s.at[k])
+    for k in range(2):
+        x_gated[k].arrive()
+        att = dot(r.emit_w[...].reshape(512, 128), r.gated_r[k].reshape(128, 128), 1)
+        r.att_s[k] = att.astype(BF16).reshape(8, 64, 128)
+        x_att[k].start()
+    for k in range(2):
+        x_att[k].arrive()
+        r.attx_s[k] = jnp.sum(r.att_r[k].astype(F32), axis=0).astype(BF16)
+        x_attx[k].start()
+    added = []
+    for k in range(2):
+        x_attx[k].arrive()
+        added.append(jnp.sum(r.attx_r[k].astype(F32), axis=0))
+    two = r.blk[...].astype(F32) + jnp.concatenate(added, axis=1)
     r.two[...] = two
     r.dev_s[...] = block_stats(two, r.st2).astype(BF16)
     x_dev = Exchange(gq, same(r.dev_s), slots(r.dev_r), r.dev_r, s.dev2)
@@ -562,20 +588,31 @@
 
     x_look.arrive()
     x_acc.arrive()
-    up = dot(mixed(0), r.look_w[...].reshape(512, 512))
-    r.up_s[...] = up.astype(BF16).reshape(8, 32, 512)
-    x_up = Exchange(gz, lambda i: r.up_s.at[i], slots(r.up_r), r.up_r, s.up)
-    x_up.start()
-    rec = dot(mixed(1), r.acc_w[...].reshape(512, 128)).T
-    r.rec_s[...] = rec.astype(BF16).reshape(8, 16, 256)
+    x_up = halves(gz, "up", lambda k, i: r.up_s.at[k, i])
+    x_units = halves(gz, "units", lambda k, i: r.units_s.at[k])
+    x_val = halves(gq, "val", lambda k, i: r.val_s.at[k, i])
+    x_valx = halves(gx, "valx", lambda k, i: r.valx_s.at[k])
+    for k in range(2):
+        up = dot(mixed(0, k), r.look_w[...].reshape(512, 512))
+        r.up_s[k] = up.astype(BF16).reshape(8, 16, 512)
+        x_up[k].start()
+    for k in range(2):
+        x_up[k].arrive()
+        up = jnp.maximum(jnp.sum(r.up_r[k].astype(F32), axis=0), 0.0)
+        up = jnp.where(jnp.logical_and(c == 1, iota(up.shape, 1) < 128), 0.0, up * up)
+        r.units_s[k] = up.astype(BF16)
+        x_units[k].start()
+    take = [dot(mixed(1, k), r.acc_w[...].reshape(512, 128)) for k in range(2)]
+    take = jnp.concatenate(take, axis=0).T
+    r.rec_s[...] = take.astype(BF16).reshape(8, 16, 256)
     x_rec = Exchange(gz, lambda i: r.rec_s.at[i], slots(r.rec_r), r.rec_r, s.rec)
     x_rec.start()
-    x_up.arrive()
-    up = jnp.maximum(jnp.sum(r.up_r[...].astype(F32), axis=0), 0.0)
-    up = jnp.where(jnp.logical_and(c == 1, iota(up.shape, 1) < 128), 0.0, up * up)
-    r.units_s[...] = up.astype(BF16)
-    x_units = Exchange(gz, same(r.units_s), slots(r.units_r), r.units_r, s.units)
-    x_units.start()
+    x_down.arrive()
+    for k in range(2):
+        x_units[k].arrive()
+        value = dot(r.down_w[...].reshape(512, 512), r.units_r[k].reshape(128, 512), 1)
+        r.val_s[k] = value.astype(BF16).reshape(8, 64, 128)
+        x_val[k].start()
     x_rec.arrive()
     r.sig_s[...] = jax.nn.sigmoid(jnp.sum(r.rec_r[...].astype(F32), axis=0))
 
@@ -600,29 +637,27 @@
         def _():
             pltpu.make_async_copy(r.sig_s, r.sig_r.at[lax.rem(z, NX)], s.sig.at[1]).start()
 
-    x_down.arrive()
-    x_units.arrive()
-    val = dot(r.down_w[...].reshape(512, 512), r.units_r[...].reshape(256, 512), 1)
-    r.val_s[...] = val.astype(BF16).reshape(8, 64, 256)
-    x_val = Exchange(gq, lambda i: r.val_s.at[i], slots(r.val_r), r.val_r, s.val)
-    x_val.start()
     x_new.arrive()
     for k in range(16):
         tile = r.state_n[k // 2].astype(F32)[(k % 2) * 32 : (k % 2) * 32 + 32]
         r.states_o[k, 0:32] = tile[:, 0:64].astype(BF16)
         r.states_o[k, 32:64] = tile[:, 64:128].astype(BF16)
-    x_val.arrive()
-    r.valx_s[...] = jnp.sum(r.val_r[...].astype(F32), axis=0).astype(BF16)
-    x_valx = Exchange(gx, same(r.valx_s), slots(r.valx_r), r.valx_r, s.valx)
-    x_valx.start()
+    for k in range(2):
+        x_val[k].arrive()
+        r.valx_s[k] = jnp.sum(r.val_r[k].astype(F32), axis=0).astype(BF16)
+        x_valx[k].start()
     pltpu.make_async_copy(r.sig_r, r.sig_r, s.sig.at[1]).wait()
-    x_valx.arrive()
-    value = jnp.sum(r.valx_r[...].astype(F32), axis=0)
+    value = []
+    for k in range(2):
+        x_valx[k].arrive()
+        value.append(jnp.sum(r.valx_r[k].astype(F32), axis=0))
+    value = jnp.concatenate(value, axis=1)
     result = r.two[...] + r.sig_r[...].reshape(64, 256) * value
     r.out[...] = jnp.where(slot < length, result, 0.0).T
     for k in range(64):
-        first = (k // 2 % NZ) * 32 + (k // 16) * 2 + k % 2
-        r.hidden_o[k] = r.out[pl.ds(first, 4, stride=8), :]
+        first = (k // 2 % NZ) * 16 + (k // 16) * 2 + k % 2
+        r.hidden_o[k, 0:2] = r.out[pl.ds(first, 2, stride=8), :]
+        r.hidden_o[k, 2:4] = r.out[pl.ds(first + 128, 2, stride=8), :]
 
     for k in range(4):
 
@@ -631,8 +666,9 @@
             far_copy(k).wait_send()
 
     for x in (
-        x_meta, x_prm, x_edges, x_state, x_low, x_maps, x_emit, x_look, x_acc, x_down, x_emb, x_zstate, x_stream,
-        x_stats, x_part, x_gated, x_new, x_att, x_attx, x_dev, x_stats2, x_up, x_rec, x_units, x_val, x_valx,
+        x_meta, x_prm, x_edges, x_state, x_low, x_maps, x_emit, x_look, x_acc, x_down, x_emb,
+        x_zstate, x_stream, x_stats, x_new, x_dev, x_stats2, x_rec, *x_part, *x_gated, *x_att,
+        *x_attx, *x_up, *x_units, *x_val, *x_valx,
     ):
         x.drain()
 
@@ -671,6 +707,7 @@
         out_specs=[VM] * 3,
         scratch_shapes=[pltpu.VMEM(shape, dtype) for _, shape, dtype in SCRATCH]
         + [DMA((2,)) for _ in SEMS]
+        + [DMA((2, 2)) for _ in HALVES]
         + [DMA((2,)), DMA(()), DMA(()), DMA((len(LOCAL),))]
         + [
             (pltpu.SMEM if n < 3 else pltpu.VMEM)(shape, dtype)

time: 102 us -> 97.1 us (0.952)
  Pallas kernels: 95.4 us -> 90.3 us
    pallas_call x1, Pallas kernels: 95.4 us -> 90.3 us  [local(): pl.pallas_call(kernel, out_shape=[jax.ShapeDtypeStruct((64, 4, 64), F32),...]
where the time goes in v4:
time: 97.1 us; the launch traced here: 96.9 us
  Pallas kernels  90.3 us (93%)
  local copies, waits for them, and re-layouts  4.61 us (5%)
  between operations  1.94 us (2%)
    pallas_call x1, Pallas kernels, local(): pl.pallas_call(kernel, out_shape=[jax.ShapeDtypeStruct((64, 4, 64), F32),...  90.3 us
    unnamed x3, local copies, waits for them, and re-layouts  4.61 us

profile of v4, /device:TPU:1, one launch (start us, length us, event | category | flops | bytes accessed | tf_op | source)
XLA Modules:
  0.0 96.9 jit_solution(14478252204810297955)
XLA Ops:
  1.9 90.3 %layer.1 = (f32[64,4,64]{2,1,0:T(4,128)}, bf16[2,64,64]{2,1,0:T(8,128)(2,1)}, bf16[16,64,64]{2,1,0:T(8,128)(2,1)}) custom-call(s32[1,4]{1,0:T(1,128)} %refs_0_.1, s32[1]{0:T(128)S(6)} %copy.27.refs_1_, s32[1]{0:T(128)S(6)} %copy.28.refs_2_, f32[2,64]{1,0:T(2,128)} %refs_3_.1, f32[2,64]{1,0:T(2,128)} %refs_4_.1, f32[5,64]{1,0:T(8,128)} %refs_5_.1, ...), custom_call_target="tpu_custom_call" | custom-call | tf_op jit(solution)/shard_map/layer/pallas_call | solution.py:699
  92.3 1.6 %copy.29 = f32[64,4,64]{2,1,0:T(4,128)} copy(f32[64,4,64]{2,1,0:T(4,128)} %get-tuple-element.12) | data formatting | bytes 131072
  93.8 1.4 %copy.30 = bf16[2,64,64]{2,1,0:T(8,128)(2,1)} copy(bf16[2,64,64]{2,1,0:T(8,128)(2,1)} %get-tuple-element.13) | data formatting | bytes 32768
  95.2 1.7 %copy.31 = bf16[1,16,64,64]{3,2,1,0:T(8,128)(2,1)} copy(bf16[1,16,64,64]{3,2,1,0:T(8,128)(2,1)} %bitcast.8) | data formatting | bytes 262144

commit v5 on v4

--- a/solution.py
+++ b/solution.py
@@ -212,10 +212,10 @@
     ("attx_s", (2, 64, 128), BF16),
     ("attx_r", (2, NX, 64, 128), BF16),
     ("two", (64, 256), F32),
-    ("dev_s", (64, 256), BF16),
-    ("st2", (2, 256), F32),
-    ("st2_r", (64, 2, 256), F32),
-    ("dev_r", (8, 64, 256), BF16),
+    ("dev2_s", (2, 64, 128), BF16),
+    ("stats2_s", (2, 2, 128), F32),
+    ("stats2_r", (2, 64, 2, 128), F32),
+    ("dev2_r", (2, 8, 64, 128), BF16),
     ("up_s", (2, 8, 16, 512), BF16),
     ("up_r", (2, 8, 16, 512), BF16),
     ("rec_s", (8, 16, 256), BF16),
@@ -232,9 +232,11 @@
 ]
 SEMS = [
     "meta", "prm", "edges", "state", "zstate", "low", "maps", "emit", "look", "acc", "down", "emb",
-    "stats", "stream", "new", "stats2", "dev2", "rec",
+    "stats", "stream", "new", "rec",
 ]
-HALVES = ["part", "gated", "att", "attx", "up", "units", "val", "valx"]
+HALVES = [
+    "part", "gated", "att", "attx", "dev2", "stats2", "up", "units", "val", "valx",
+]
 
 
 class Refs:
@@ -423,9 +425,12 @@
     x_prm.arrive()
     prm = jnp.concatenate([r.prm_r[2 * k] + r.prm_r[2 * k + 1] for k in range(NY)], axis=1)
 
+    def edge_rows(k):
+        return jnp.concatenate([r.edges_f[:, i * 2 + k, :] for i in range(NY)], axis=1)
+
     def shifted(normed, k, first):
         now = normed.astype(F32).reshape(2, 8, 2, 8, 512)
-        edge = jnp.concatenate([r.edges_f[:, i * 2 + k, :] for i in range(NY)], axis=1)
+        edge = edge_rows(k)
         before = [
             jnp.concatenate([edge.reshape(8, 1, 8, 512), now[0, :, :1]], axis=1).reshape(128, 512),
             jnp.concatenate([now[0, :, 1:], now[1, :, :1]], axis=1).reshape(128, 512),
@@ -565,26 +570,39 @@
         x_att[k].arrive()
         r.attx_s[k] = jnp.sum(r.att_r[k].astype(F32), axis=0).astype(BF16)
         x_attx[k].start()
-    added = []
+    x_dev = halves(gq, "dev2", lambda k, i: r.dev2_s.at[k])
+    x_stats2 = halves(gb, "stats2", lambda k, i: r.stats2_s.at[k])
     for k in range(2):
         x_attx[k].arrive()
-        added.append(jnp.sum(r.attx_r[k].astype(F32), axis=0))
-    two = r.blk[...].astype(F32) + jnp.concatenate(added, axis=1)
-    r.two[...] = two
-    r.dev_s[...] = block_stats(two, r.st2).astype(BF16)
-    x_dev = Exchange(gq, same(r.dev_s), slots(r.dev_r), r.dev_r, s.dev2)
-    x_dev.start()
-    x_stats2 = Exchange(gb, same(r.st2), slots(r.st2_r), r.st2_r, s.stats2)
-    x_stats2.start()
-    x_dev.arrive()
-    x_stats2.arrive()
-    mean, var = join(r.st2_r, 64.0, 4096.0)
-    scale = lax.rsqrt(var + EPS_LN)
-    blocks = []
-    for n in range(8):
-        off = r.st2_r[batch_of(n // 2, z, n % 2)][0:1] - mean
-        blocks.append((r.dev_r[n].astype(F32) + off) * scale)
-    mixed = shifted(layer(jnp.concatenate(blocks, axis=0), 1), 1, 9)
+        part = slice(k * 128, k * 128 + 128)
+        two = r.blk[:, part].astype(F32) + jnp.sum(r.attx_r[k].astype(F32), axis=0)
+        r.two[:, part] = two
+        r.dev2_s[k] = block_stats(two, r.stats2_s.at[k]).astype(BF16)
+        x_dev[k].start()
+        x_stats2[k].start()
+    edge = edge_rows(1).reshape(8, 1, 8, 512)
+    now, delta = [], []
+
+    def second(k):
+        x_dev[k].arrive()
+        x_stats2[k].arrive()
+        mean, var = join(r.stats2_r.at[k], 64.0, 4096.0)
+        scale = lax.rsqrt(var + EPS_LN)
+        blocks = []
+        for n in range(8):
+            off = r.stats2_r[k, batch_of(n // 2, z, n % 2)][0:1] - mean
+            blocks.append((r.dev2_r[k, n].astype(F32) + off) * scale)
+        normed = jnp.concatenate(blocks, axis=0).T * prm[1:2] + prm[3:4]
+        normed = normed.astype(BF16).astype(F32)
+        r.norm_t[:, k * 128 : k * 128 + 128] = normed.T
+        now.append(normed)
+        split_now = [n.reshape(8, 2, 8, 512) for n in now]
+        ahead = edge if k == 0 else split_now[0][:, 1:]
+        before = jnp.concatenate([ahead, split_now[k][:, :1]], axis=1).reshape(128, 512)
+        delta.append(before - normed)
+
+    def mixed(n, k):
+        return (now[k] + delta[k] * prm[9 + n : 10 + n]).astype(BF16)
 
     x_look.arrive()
     x_acc.arrive()
@@ -593,6 +611,7 @@
     x_val = halves(gq, "val", lambda k, i: r.val_s.at[k, i])
     x_valx = halves(gx, "valx", lambda k, i: r.valx_s.at[k])
     for k in range(2):
+        second(k)
         up = dot(mixed(0, k), r.look_w[...].reshape(512, 512))
         r.up_s[k] = up.astype(BF16).reshape(8, 16, 512)
         x_up[k].start()
@@ -602,6 +621,8 @@
         up = jnp.where(jnp.logical_and(c == 1, iota(up.shape, 1) < 128), 0.0, up * up)
         r.units_s[k] = up.astype(BF16)
         x_units[k].start()
+    mine = r.norm_t[rows(q * 64, 64), :].astype(BF16)
+    r.new_edges_o[1] = dot(last, mine, 1).astype(BF16)
     take = [dot(mixed(1, k), r.acc_w[...].reshape(512, 128)) for k in range(2)]
     take = jnp.concatenate(take, axis=0).T
     r.rec_s[...] = take.astype(BF16).reshape(8, 16, 256)
@@ -667,7 +688,7 @@
 
     for x in (
         x_meta, x_prm, x_edges, x_state, x_low, x_maps, x_emit, x_look, x_acc, x_down, x_emb,
-        x_zstate, x_stream, x_stats, x_new, x_dev, x_stats2, x_rec, *x_part, *x_gated, *x_att,
+        x_zstate, x_stream, x_stats, x_new, x_rec, *x_dev, *x_stats2, *x_part, *x_gated, *x_att,
         *x_attx, *x_up, *x_units, *x_val, *x_valx,
     ):
         x.drain()

time: 97.1 us -> 95.7 us (0.986)
  Pallas kernels: 90.3 us -> 88.9 us
    pallas_call x1, Pallas kernels: 90.3 us -> 88.9 us  [local(): pl.pallas_call(kernel, out_shape=[jax.ShapeDtypeStruct((64, 4, 64), F32),...]
where the time goes in v5:
time: 95.7 us; the launch traced here: 95.5 us
  Pallas kernels  88.9 us (93%)
  local copies, waits for them, and re-layouts  4.61 us (5%)
  between operations  1.94 us (2%)
    pallas_call x1, Pallas kernels, local(): pl.pallas_call(kernel, out_shape=[jax.ShapeDtypeStruct((64, 4, 64), F32),...  88.9 us
    unnamed x3, local copies, waits for them, and re-layouts  4.61 us

profile of v5, /device:TPU:1, one launch (start us, length us, event | category | flops | bytes accessed | tf_op | source)
XLA Modules:
  0.0 95.5 jit_solution(12835257850432843782)
XLA Ops:
  1.9 88.9 %layer.1 = (f32[64,4,64]{2,1,0:T(4,128)}, bf16[2,64,64]{2,1,0:T(8,128)(2,1)}, bf16[16,64,64]{2,1,0:T(8,128)(2,1)}) custom-call(s32[1,4]{1,0:T(1,128)} %refs_0_.1, s32[1]{0:T(128)S(6)} %copy.27.refs_1_, s32[1]{0:T(128)S(6)} %copy.28.refs_2_, f32[2,64]{1,0:T(2,128)} %refs_3_.1, f32[2,64]{1,0:T(2,128)} %refs_4_.1, f32[5,64]{1,0:T(8,128)} %refs_5_.1, ...), custom_call_target="tpu_custom_call" | custom-call | tf_op jit(solution)/shard_map/layer/pallas_call | solution.py:720
  90.9 1.6 %copy.29 = f32[64,4,64]{2,1,0:T(4,128)} copy(f32[64,4,64]{2,1,0:T(4,128)} %get-tuple-element.12) | data formatting | bytes 131072
  92.4 1.4 %copy.30 = bf16[2,64,64]{2,1,0:T(8,128)(2,1)} copy(bf16[2,64,64]{2,1,0:T(8,128)(2,1)} %get-tuple-element.13) | data formatting | bytes 32768
  93.8 1.7 %copy.31 = bf16[1,16,64,64]{3,2,1,0:T(8,128)(2,1)} copy(bf16[1,16,64,64]{3,2,1,0:T(8,128)(2,1)} %bitcast.8) | data formatting | bytes 262144

commit v6 on v5

--- a/solution.py
+++ b/solution.py
@@ -384,7 +384,7 @@
     length = tok_rows[4:5].astype(jnp.int32)
 
     vocab_in.wait()
-    step = 4096
+    step = 8192
 
     def look_up(k, acc):
         base = pl.multiple_of(k * step, step)
@@ -461,16 +461,14 @@
 
     def layer(x, k):
         normed = (x.T * prm[k : k + 1] + prm[2 + k : 3 + k]).astype(BF16)
-        r.norm_t[...] = normed.astype(F32).T
-        mine = r.norm_t[rows(q * 64, 64), :].astype(BF16)
-        r.new_edges_o[k] = dot(last, mine, 1).astype(BF16)
         return normed
 
     x_stream.arrive()
     x_stats.arrive()
     mean, var = join(r.st_r, 64.0, 4096.0)
     scaled = (r.stream_r[...].astype(F32).reshape(512, 256) - mean) * lax.rsqrt(var + EPS_LN)
-    mixed = shifted(layer(scaled, 0), 0, 4)
+    normed = layer(scaled, 0)
+    mixed = shifted(normed, 0, 4)
     x_maps.arrive()
     x_low.arrive()
     x_part = halves(gz, "part", lambda k, i: r.part_s.at[k, :, rows(i * 16, 16)])
@@ -481,6 +479,10 @@
         x_part[k].start()
     for x in (x_emit, x_look, x_acc, x_down):
         x.start()
+
+    r.norm_t[...] = normed.astype(F32).T
+    mine = r.norm_t[rows(q * 64, 64), :].astype(BF16)
+    r.new_edges_o[0] = dot(last, mine, 1).astype(BF16)
 
     x_zstate.arrive()
     left = iota((32, 128), 1) < 64
@@ -539,6 +541,14 @@
         r.gated_s[k] = (grouped * (gate * jax.nn.sigmoid(gate))).astype(BF16)
         x_gated[k].start()
 
+    x_emit.arrive()
+    x_att = halves(gq, "att", lambda k, i: r.att_s.at[k, i])
+    x_attx = halves(gx, "attx", lambda k, i: r.attx_s.at[k])
+    for k in range(2):
+        x_gated[k].arrive()
+        att = dot(r.emit_w[...].reshape(512, 128), r.gated_r[k].reshape(128, 128), 1)
+        r.att_s[k] = att.astype(BF16).reshape(8, 64, 128)
+        x_att[k].start()
     tail, keys = jnp.ones((8, 128), F32), []
     for j in range(3, -1, -1):
         keys.append(jnp.where(alive[j], key[j] * tail, 0.0))
@@ -558,14 +568,6 @@
     x_new = Exchange(gq, lambda i: r.new_s.at[i], lambda m: r.state_n.at[m], r.state_n, s.new)
     x_new.start()
 
-    x_emit.arrive()
-    x_att = halves(gq, "att", lambda k, i: r.att_s.at[k, i])
-    x_attx = halves(gx, "attx", lambda k, i: r.attx_s.at[k])
-    for k in range(2):
-        x_gated[k].arrive()
-        att = dot(r.emit_w[...].reshape(512, 128), r.gated_r[k].reshape(128, 128), 1)
-        r.att_s[k] = att.astype(BF16).reshape(8, 64, 128)
-        x_att[k].start()
     for k in range(2):
         x_att[k].arrive()
         r.attx_s[k] = jnp.sum(r.att_r[k].astype(F32), axis=0).astype(BF16)

time: 95.7 us -> 93 us (0.972)
  Pallas kernels: 88.9 us -> 86.2 us
    pallas_call x1, Pallas kernels: 88.9 us -> 86.2 us  [local(): pl.pallas_call(kernel, out_shape=[jax.ShapeDtypeStruct((64, 4, 64), F32),...]
where the time goes in v6:
time: 93 us; the launch traced here: 92.8 us
  Pallas kernels  86.2 us (93%)
  local copies, waits for them, and re-layouts  4.61 us (5%)
  between operations  1.94 us (2%)
    pallas_call x1, Pallas kernels, local(): pl.pallas_call(kernel, out_shape=[jax.ShapeDtypeStruct((64, 4, 64), F32),...  86.2 us
    unnamed x3, local copies, waits for them, and re-layouts  4.61 us

profile of v6, /device:TPU:1, one launch (start us, length us, event | category | flops | bytes accessed | tf_op | source)
XLA Modules:
  0.0 92.8 jit_solution(16473853654895434120)
XLA Ops:
  1.9 86.2 %layer.1 = (f32[64,4,64]{2,1,0:T(4,128)}, bf16[2,64,64]{2,1,0:T(8,128)(2,1)}, bf16[16,64,64]{2,1,0:T(8,128)(2,1)}) custom-call(s32[1,4]{1,0:T(1,128)} %refs_0_.1, s32[1]{0:T(128)S(6)} %copy.27.refs_1_, s32[1]{0:T(128)S(6)} %copy.28.refs_2_, f32[2,64]{1,0:T(2,128)} %refs_3_.1, f32[2,64]{1,0:T(2,128)} %refs_4_.1, f32[5,64]{1,0:T(8,128)} %refs_5_.1, ...), custom_call_target="tpu_custom_call" | custom-call | tf_op jit(solution)/shard_map/layer/pallas_call | solution.py:722
  88.1 1.6 %copy.29 = f32[64,4,64]{2,1,0:T(4,128)} copy(f32[64,4,64]{2,1,0:T(4,128)} %get-tuple-element.12) | data formatting | bytes 131072
  89.7 1.4 %copy.30 = bf16[2,64,64]{2,1,0:T(8,128)(2,1)} copy(bf16[2,64,64]{2,1,0:T(8,128)(2,1)} %get-tuple-element.13) | data formatting | bytes 32768
  91.1 1.7 %copy.31 = bf16[1,16,64,64]{3,2,1,0:T(8,128)(2,1)} copy(bf16[1,16,64,64]{3,2,1,0:T(8,128)(2,1)} %bitcast.8) | data formatting | bytes 262144

commit v7 on v6

--- a/solution.py
+++ b/solution.py
@@ -384,7 +384,7 @@
     length = tok_rows[4:5].astype(jnp.int32)
 
     vocab_in.wait()
-    step = 8192
+    step = 16384
 
     def look_up(k, acc):
         base = pl.multiple_of(k * step, step)

time: 93 us -> 94.5 us (1.016)
  Pallas kernels: 86.2 us -> 87.8 us
    pallas_call x1, Pallas kernels: 86.2 us -> 87.8 us  [local(): pl.pallas_call(kernel, out_shape=[jax.ShapeDtypeStruct((64, 4, 64), F32),...]
where the time goes in v7:
time: 94.5 us; the launch traced here: 94.3 us
  Pallas kernels  87.8 us (93%)
  local copies, waits for them, and re-layouts  4.61 us (5%)
  between operations  1.94 us (2%)
    pallas_call x1, Pallas kernels, local(): pl.pallas_call(kernel, out_shape=[jax.ShapeDtypeStruct((64, 4, 64), F32),...  87.8 us
    unnamed x3, local copies, waits for them, and re-layouts  4.61 us

profile of v7, /device:TPU:1, one launch (start us, length us, event | category | flops | bytes accessed | tf_op | source)
XLA Modules:
  0.0 94.3 jit_solution(1504720822989976628)
XLA Ops:
  1.9 87.8 %layer.1 = (f32[64,4,64]{2,1,0:T(4,128)}, bf16[2,64,64]{2,1,0:T(8,128)(2,1)}, bf16[16,64,64]{2,1,0:T(8,128)(2,1)}) custom-call(s32[1,4]{1,0:T(1,128)} %refs_0_.1, s32[1]{0:T(128)S(6)} %copy.27.refs_1_, s32[1]{0:T(128)S(6)} %copy.28.refs_2_, f32[2,64]{1,0:T(2,128)} %refs_3_.1, f32[2,64]{1,0:T(2,128)} %refs_4_.1, f32[5,64]{1,0:T(8,128)} %refs_5_.1, ...), custom_call_target="tpu_custom_call" | custom-call | tf_op jit(solution)/shard_map/layer/pallas_call | solution.py:722
  89.7 1.6 %copy.29 = f32[64,4,64]{2,1,0:T(4,128)} copy(f32[64,4,64]{2,1,0:T(4,128)} %get-tuple-element.12) | data formatting | bytes 131072
  91.3 1.4 %copy.30 = bf16[2,64,64]{2,1,0:T(8,128)(2,1)} copy(bf16[2,64,64]{2,1,0:T(8,128)(2,1)} %get-tuple-element.13) | data formatting | bytes 32768
  92.6 1.7 %copy.31 = bf16[1,16,64,64]{3,2,1,0:T(8,128)(2,1)} copy(bf16[1,16,64,64]{3,2,1,0:T(8,128)(2,1)} %bitcast.8) | data formatting | bytes 262144
